TPU v7x, 128 devices: a whole 4x4x4 slice. The times are simulated.
128 devices in a mesh: prow: 16 (over x, z), pcol: 8 (over y, core).
Axes of the slice: x: 4, y: 4, z: 4, core: 2. Of those that a mesh axis runs over, the one named last changes fastest.
Arguments:
- rhs: float32 [31, 64, 2048], P(None, None, 'prow'), may hold values from -6 to 6
- factor: bfloat16 [98, 2048, 2048], P(None, 'prow', 'pcol'), may hold values from -0.03125 to 0.03125
- inverse: bfloat16 [31, 2048, 2048], P(None, 'pcol', 'prow')
- pattern: int32 [98], replicated, may hold values 0 or 1
Outputs:
- solution: float32 [31, 64, 2048], P(None, None, 'prow')
- forward_solution: float32 [31, 64, 2048], P(None, None, 'pcol')
All inputs are finite; a program needn't handle non-finite values.
Results may differ from a plain program's by a relative error of at most 0.011.
Values sent between devices are 32-bit elements; how exact they have to be, the bound alone decides.
No kernel may reach another device: no remote copies, remote signals or barrier semaphores. Data moves between devices by JAX's collectives and lax.ppermute only.
A program may use at most 64 MiB of HBM per device.

v0:
```python
import jax
import jax.numpy as jnp
from jax import lax
from jax.sharding import PartitionSpec as P

LEV = 5


def block_start(tree_depth):
    return (tree_depth - 2) * 2**tree_depth + 2


def sum_columns(values):
    result = lax.psum(values, "pcol")
    return lax.optimization_barrier(result)


def sum_rows(values):
    result = lax.psum(values, "prow")
    return lax.optimization_barrier(result)


def per_device(rhs, factor, inverse, pattern):
    live = pattern.astype(jnp.float32)
    partial_value = jnp.zeros(rhs.shape, jnp.float32)
    forward_levels = [None] * LEV
    for tree_depth in range(LEV - 1, -1, -1):
        first = 2**tree_depth - 1
        count = 2**tree_depth
        residual = rhs[first : first + count]
        if tree_depth < LEV - 1:
            residual = residual - sum_columns(partial_value[first : first + count])
        rounded = residual.astype(jnp.bfloat16)
        pieces = jnp.einsum(
            "nrc,nwc->nrw",
            rounded,
            inverse[first : first + count],
            preferred_element_type=jnp.float32,
        )
        forward = sum_rows(pieces)
        forward_levels[tree_depth] = forward
        narrow = forward.astype(jnp.bfloat16)
        if tree_depth > 0:
            start = block_start(tree_depth)
            weights = live[start : start + count * tree_depth].reshape(count, tree_depth)
            for upward in range(1, tree_depth + 1):
                blocks = factor[start + upward - 1 : start + count * tree_depth : tree_depth]
                terms = jnp.einsum(
                    "nrc,nwc->nrw", narrow, blocks, preferred_element_type=jnp.float32
                )
                terms = terms * weights[:, upward - 1][:, None, None]
                groups = count >> upward
                terms = terms.reshape((groups, 2**upward) + terms.shape[1:]).sum(axis=1)
                target = 2 ** (tree_depth - upward) - 1
                partial_value = partial_value.at[target : target + groups].add(terms)
    solved = [None] * LEV
    solved_narrow = [None] * LEV
    for tree_depth in range(LEV):
        first = 2**tree_depth - 1
        count = 2**tree_depth
        target_vec = forward_levels[tree_depth]
        if tree_depth > 0:
            start = block_start(tree_depth)
            weights = live[start : start + count * tree_depth].reshape(count, tree_depth)
            gathered = jnp.zeros(target_vec.shape, jnp.float32)
            for upward in range(1, tree_depth + 1):
                blocks = factor[start + upward - 1 : start + count * tree_depth : tree_depth]
                above = jnp.repeat(solved_narrow[tree_depth - upward], 2**upward, axis=0)
                terms = jnp.einsum(
                    "nrw,nwc->nrc", above, blocks, preferred_element_type=jnp.float32
                )
                gathered = gathered + terms * weights[:, upward - 1][:, None, None]
            target_vec = target_vec - sum_rows(gathered)
        rounded = target_vec.astype(jnp.bfloat16)
        pieces = jnp.einsum(
            "nrw,nwc->nrc",
            rounded,
            inverse[first : first + count],
            preferred_element_type=jnp.float32,
        )
        solution = sum_columns(pieces)
        solved[tree_depth] = solution
        solved_narrow[tree_depth] = solution.astype(jnp.bfloat16)
    return (jnp.concatenate(solved, axis=0), jnp.concatenate(forward_levels, axis=0))


def solution(mesh):
    in_specs = (P(None, None, "prow"), P(None, "prow", "pcol"), P(None, "pcol", "prow"), P())
    out_specs = (P(None, None, "prow"), P(None, None, "pcol"))
    return jax.shard_map(
        per_device, mesh=mesh, in_specs=in_specs, out_specs=out_specs, check_vma=False
    )
```

profile of v0, /device:TPU:1, one launch (start us, length us, event | category | flops | bytes accessed | tf_op | source)
XLA Modules:
  0.0 1292.6 jit_solution(4972876091253898043)
XLA Ops:
  7.2 2.8 fusion.20
  10.3 0.2 slice_reduce_fusion
  10.5 90.3 %all-reduce.18.cloned.1.call-done = f32[16,64,256]{2,1,0:T(8,128)} async-done(((f32[16,64,256]{2,1,0:T(8,128)}), f32[16,64,256]{2,1,0:T(8,128)}) %all-reduce.18.cloned.1.call-update) | async-done | bytes 1048592 | tf_op jit(solution)/shard_map/psum | solution.py:19
  100.8 1.3 convert_element_type.57
  102.1 1.7 bitcast_reduce_fusion.2
  103.8 1.7 bitcast_reduce_fusion.1
  105.5 1.7 bitcast_reduce_fusion
  107.3 1.7 fusion.5
  109.1 0.7 slice.423
  109.9 58.5 %all-reduce.20.cloned.1.call-done = f32[8,64,128]{2,1,0:T(8,128)} async-done(((f32[8,64,128]{2,1,0:T(8,128)}), f32[8,64,128]{2,1,0:T(8,128)}) %all-reduce.20.cloned.1.call-update) | async-done | bytes 262160 | tf_op jit(solution)/shard_map/psum | solution.py:14
  168.4 2.3 fusion.31
  171.2 86.5 %all-reduce.22.cloned.1.call-done = f32[8,64,256]{2,1,0:T(8,128)} async-done(((f32[8,64,256]{2,1,0:T(8,128)}), f32[8,64,256]{2,1,0:T(8,128)}) %all-reduce.22.cloned.1.call-update) | async-done | bytes 524304 | tf_op jit(solution)/shard_map/psum | solution.py:19
  257.7 1.6 bitcast_reduce_fusion.4
  259.4 1.5 bitcast_reduce_fusion.3
  261.0 0.7 slice.426
  261.7 57.9 %all-reduce.24.cloned.1.call-done = f32[4,64,128]{2,1,0:T(8,128)} async-done(((f32[4,64,128]{2,1,0:T(8,128)}), f32[4,64,128]{2,1,0:T(8,128)}) %all-reduce.24.cloned.1.call-update) | async-done | bytes 131088 | tf_op jit(solution)/shard_map/psum | solution.py:14
  319.6 2.0 fusion.45
  322.0 85.7 %all-reduce.26.cloned.1.call-done = f32[4,64,256]{2,1,0:T(8,128)} async-done(((f32[4,64,256]{2,1,0:T(8,128)}), f32[4,64,256]{2,1,0:T(8,128)}) %all-reduce.26.cloned.1.call-update) | async-done | bytes 262160 | tf_op jit(solution)/shard_map/psum | solution.py:19
  407.7 1.3 bitcast_reduce_fusion.5
  409.0 0.6 fusion.76
  409.8 1.3 fusion.7
  411.1 56.6 %all-reduce.28.cloned.1.call-done = f32[2,64,128]{2,1,0:T(8,128)} async-done(((f32[2,64,128]{2,1,0:T(8,128)}), f32[2,64,128]{2,1,0:T(8,128)}) %all-reduce.28.cloned.1.call-update) | async-done | bytes 65552 | tf_op jit(solution)/shard_map/psum | solution.py:14
  467.7 1.8 fusion.57
  469.6 1.2 fusion.8
  470.8 82.9 %all-reduce.30.cloned.1.call-done = f32[2,64,256]{2,1,0:T(8,128)} async-done(((f32[2,64,256]{2,1,0:T(8,128)}), f32[2,64,256]{2,1,0:T(8,128)}) %all-reduce.30.cloned.1.call-update) | async-done | bytes 131088 | tf_op jit(solution)/shard_map/psum | solution.py:19
  553.8 1.1 fusion.9
  554.9 22.7 %psum.133 = f32[1,64,128]{2,1,0:T(8,128)S(1)} all-reduce(f32[1,64,128]{2,1,0:T(8,128)S(1)} %fusion.71), channel_id=1, replica_groups=mesh['prow'=16,'pcol'=8] {'pcol'}, use_global_device_ids=true, to_apply=%region_17.0 | all-reduce | flops 8192 | bytes 65536 | tf_op jit(solution)/shard_map/psum | solution.py:14
  577.7 1.6 convolution_bitcast_fusion
  579.4 78.9 %all-reduce.32.cloned.1.call-done = f32[1,64,256]{2,1,0:T(8,128)} async-done(((f32[1,64,256]{2,1,0:T(8,128)}), f32[1,64,256]{2,1,0:T(8,128)}) %all-reduce.32.cloned.1.call-update) | async-done | bytes 65552 | tf_op jit(solution)/shard_map/psum | solution.py:19
  658.3 1.0 convolution_bitcast_fusion.1
  659.3 22.7 %psum.135 = f32[1,64,128]{2,1,0:T(8,128)S(1)} all-reduce(f32[1,64,128]{2,1,0:T(8,128)S(1)} %convolution_bitcast_fusion.1), channel_id=1, replica_groups=mesh['prow'=16,'pcol'=8] {'pcol'}, use_global_device_ids=true, to_apply=%region_19.0 | all-reduce | flops 8192 | bytes 65536 | tf_op jit(solution)/shard_map/psum | solution.py:14
  682.1 1.7 convolution_multiply_fusion.18
  683.8 80.5 %all-reduce.34.cloned.1.call-done = f32[2,64,256]{2,1,0:T(8,128)} async-done(((f32[2,64,256]{2,1,0:T(8,128)}), f32[2,64,256]{2,1,0:T(8,128)}) %all-reduce.34.cloned.1.call-update) | async-done | bytes 131088 | tf_op jit(solution)/shard_map/psum | solution.py:19
  764.3 1.8 fusion.55
  766.2 58.4 %all-reduce.36.cloned.1.call-done = f32[2,64,128]{2,1,0:T(8,128)} async-done(((f32[2,64,128]{2,1,0:T(8,128)}), f32[2,64,128]{2,1,0:T(8,128)}) %all-reduce.36.cloned.1.call-update) | async-done | bytes 65552 | tf_op jit(solution)/shard_map/psum | solution.py:14
  824.6 0.9 fusion.86
  825.5 1.1 convolution_multiply_fusion.12
  826.7 1.8 fusion.6
  828.6 84.3 %all-reduce.38.cloned.1.call-done = f32[4,64,256]{2,1,0:T(8,128)} async-done(((f32[4,64,256]{2,1,0:T(8,128)}), f32[4,64,256]{2,1,0:T(8,128)}) %all-reduce.38.cloned.1.call-update) | async-done | bytes 262160 | tf_op jit(solution)/shard_map/psum | solution.py:19
  912.8 1.9 fusion.43
  914.8 58.5 %all-reduce.40.cloned.1.call-done = f32[4,64,128]{2,1,0:T(8,128)} async-done(((f32[4,64,128]{2,1,0:T(8,128)}), f32[4,64,128]{2,1,0:T(8,128)}) %all-reduce.40.cloned.1.call-update) | async-done | bytes 131088 | tf_op jit(solution)/shard_map/psum | solution.py:14
  973.3 1.0 fusion.85
  974.4 1.3 convolution_multiply_fusion.10
  975.6 1.3 fusion.4
  976.9 2.1 fusion.3
  979.1 85.2 %all-reduce.42.cloned.1.call-done = f32[8,64,256]{2,1,0:T(8,128)} async-done(((f32[8,64,256]{2,1,0:T(8,128)}), f32[8,64,256]{2,1,0:T(8,128)}) %all-reduce.42.cloned.1.call-update) | async-done | bytes 524304 | tf_op jit(solution)/shard_map/psum | solution.py:19
  1064.3 2.1 fusion.29
  1066.4 59.0 %all-reduce.44.cloned.1.call-done = f32[8,64,128]{2,1,0:T(8,128)} async-done(((f32[8,64,128]{2,1,0:T(8,128)}), f32[8,64,128]{2,1,0:T(8,128)}) %all-reduce.44.cloned.1.call-update) | async-done | bytes 262160 | tf_op jit(solution)/shard_map/psum | solution.py:14
  1125.4 1.1 fusion.84
  1126.6 0.9 copy-done.5
  1127.5 1.6 convolution_multiply_fusion.3
  1129.1 1.6 fusion.2
  1130.8 1.5 fusion.1
  1132.3 2.5 fusion
  1134.9 0.6 constant_dynamic-update-slice_fusion.9
  1135.6 0.7 constant_dynamic-update-slice_fusion.8
  1136.2 0.7 constant_dynamic-update-slice_fusion.7
  1136.9 84.9 %all-reduce.46.cloned.1.call-done = f32[16,64,256]{2,1,0:T(8,128)} async-done(((f32[16,64,256]{2,1,0:T(8,128)}), f32[16,64,256]{2,1,0:T(8,128)}) %all-reduce.46.cloned.1.call-update) | async-done | bytes 1048592 | tf_op jit(solution)/shard_map/psum | solution.py:19
  1221.8 2.7 fusion.18
  1224.5 0.8 constant_dynamic-update-slice_fusion.6
  1225.4 1.1 constant_dynamic-update-slice_fusion.5
  1226.4 57.6 %all-reduce.48.cloned.1.call-done = f32[16,64,128]{2,1,0:T(8,128)} async-done(((f32[16,64,128]{2,1,0:T(8,128)}), f32[16,64,128]{2,1,0:T(8,128)}) %all-reduce.48.cloned.1.call-update) | async-done | bytes 524304 | tf_op jit(solution)/shard_map/psum | solution.py:14
  1284.0 1.1 constant_dynamic-update-slice_fusion
  1285.1 0.9 copy-done.7
  (72 shorter events, 2.3 us)
Async XLA Ops:
  7.2 3.0 copy-start.8
  7.2 93.6 %all-reduce.18.cloned.1.call-start = ((), (), s32[]{:S(2)}) async-start(), calls=%async_computation | async-start | bytes 2097152 | tf_op jit(solution)/shard_map/psum | solution.py:19
  10.1 158.3 %all-reduce.20.cloned.1.call-start = ((), (), s32[]{:S(2)}) async-start(), calls=%async_computation.1 | async-start | bytes 524288 | tf_op jit(solution)/shard_map/psum | solution.py:14
  109.9 147.8 %all-reduce.22.cloned.1.call-start = ((), (), s32[]{:S(2)}) async-start(), calls=%async_computation.2 | async-start | bytes 1048576 | tf_op jit(solution)/shard_map/psum | solution.py:19
  170.7 148.9 %all-reduce.24.cloned.1.call-start = ((), (), s32[]{:S(2)}) async-start(), calls=%async_computation.3 | async-start | bytes 262144 | tf_op jit(solution)/shard_map/psum | solution.py:14
  257.7 152.0 %copy-start = (f32[8,64,256]{2,1,0:T(8,128)S(1)}, f32[8,64,256]{2,1,0:T(8,128)}, u32[]{:S(2)}) copy-start(f32[8,64,256]{2,1,0:T(8,128)} %all-reduce.22.cloned.1.call-done) | copy-start | bytes 1572868
  261.6 146.1 %all-reduce.26.cloned.1.call-start = ((), (), s32[]{:S(2)}) async-start(), calls=%async_computation.4 | async-start | bytes 524288 | tf_op jit(solution)/shard_map/psum | solution.py:19
  321.6 146.1 %all-reduce.28.cloned.1.call-start = ((), (), s32[]{:S(2)}) async-start(), calls=%async_computation.5 | async-start | bytes 131072 | tf_op jit(solution)/shard_map/psum | solution.py:14
  407.7 505.1 %copy-start.2 = (f32[4,64,256]{2,1,0:T(8,128)S(1)}, f32[4,64,256]{2,1,0:T(8,128)}, u32[]{:S(2)}) copy-start(f32[4,64,256]{2,1,0:T(8,128)} %all-reduce.26.cloned.1.call-done) | copy-start | bytes 786436
  409.7 144.1 %all-reduce.30.cloned.1.call-start = ((), (), s32[]{:S(2)}) async-start(), calls=%async_computation.6 | async-start | bytes 262144 | tf_op jit(solution)/shard_map/psum | solution.py:19
  469.5 188.8 %all-reduce.32.cloned.1.call-start = ((), (), s32[]{:S(2)}) async-start(), calls=%async_computation.7 | async-start | bytes 131072 | tf_op jit(solution)/shard_map/psum | solution.py:19
  579.3 185.0 %all-reduce.34.cloned.1.call-start = ((), (), s32[]{:S(2)}) async-start(), calls=%async_computation.8 | async-start | bytes 262144 | tf_op jit(solution)/shard_map/psum | solution.py:19
  683.8 140.8 %all-reduce.36.cloned.1.call-start = ((), (), s32[]{:S(2)}) async-start(), calls=%async_computation.9 | async-start | bytes 131072 | tf_op jit(solution)/shard_map/psum | solution.py:14
  766.2 146.7 %all-reduce.38.cloned.1.call-start = ((), (), s32[]{:S(2)}) async-start(), calls=%async_computation.10 | async-start | bytes 524288 | tf_op jit(solution)/shard_map/psum | solution.py:19
  828.5 144.8 %all-reduce.40.cloned.1.call-start = ((), (), s32[]{:S(2)}) async-start(), calls=%async_computation.11 | async-start | bytes 262144 | tf_op jit(solution)/shard_map/psum | solution.py:14
  914.7 149.5 %all-reduce.42.cloned.1.call-start = ((), (), s32[]{:S(2)}) async-start(), calls=%async_computation.12 | async-start | bytes 1048576 | tf_op jit(solution)/shard_map/psum | solution.py:19
  979.0 146.4 %all-reduce.44.cloned.1.call-start = ((), (), s32[]{:S(2)}) async-start(), calls=%async_computation.13 | async-start | bytes 524288 | tf_op jit(solution)/shard_map/psum | solution.py:14
  1066.4 155.4 %all-reduce.46.cloned.1.call-start = ((), (), s32[]{:S(2)}) async-start(), calls=%async_computation.14 | async-start | bytes 2097152 | tf_op jit(solution)/shard_map/psum | solution.py:19
  1126.5 1.0 copy-start.5
  1127.4 7.5 copy-start.4
  1129.0 6.5 copy-start.3
  1129.0 92.8 %copy-start.1 = (f32[16,64,256]{2,1,0:T(8,128)S(1)}, f32[16,64,256]{2,1,0:T(8,128)}, u32[]{:S(2)}) copy-start(f32[16,64,256]{2,1,0:T(8,128)} %all-reduce.18.cloned.1.call-done) | copy-start | bytes 3145732
  1134.8 149.2 %copy-start.6 = (f32[31,64,128]{2,1,0:T(8,128)S(1)}, f32[31,64,128]{2,1,0:T(8,128)}, u32[]{:S(2)}) copy-start(f32[31,64,128]{2,1,0:T(8,128)} %copy-done.5) | copy-start | bytes 3047428
  1134.9 149.1 %all-reduce.48.cloned.1.call-start = ((), (), s32[]{:S(2)}) async-start(), calls=%async_computation.15 | async-start | bytes 1048576 | tf_op jit(solution)/shard_map/psum | solution.py:14
  1285.1 1.0 copy-start.7
Sparse Core Ops, SparseCore 0:
  11.8 88.9 all-reduce.17
  110.0 58.3 all-reduce.19
  172.6 85.1 all-reduce.21
  261.8 57.7 all-reduce.23
  323.5 84.1 all-reduce.25
  410.5 57.1 all-reduce.27
  471.8 81.9 all-reduce.29
  579.5 78.7 all-reduce.31
  683.9 80.3 all-reduce.33
  767.1 57.4 all-reduce.35
  828.6 84.1 all-reduce.37
  915.6 57.6 all-reduce.39
  979.1 85.0 all-reduce.41
  1067.0 58.3 all-reduce.43
  1135.0 86.8 all-reduce.45
  1224.7 59.2 all-reduce.47
where the time goes:
time: 1300 us; the launch traced here: 1290 us
  waiting for transfers between devices  1170 us (90%)
  matrix products  51.5 us (4%)
  blocking collectives  45.5 us (4%)
  between operations  14.3 us (1%)
    psum x9, waiting for transfers between devices, sum_rows(): result = lax.psum(values, 'prow')  759 us
    psum x7, waiting for transfers between devices, sum_columns(): result = lax.psum(values, 'pcol')  406 us
    psum x2, blocking collectives, sum_columns(): result = lax.psum(values, 'pcol')  45.5 us
  transfers between devices with their start and end apart: 16, of which 16 were waited for; matrix products, arithmetic and copies ran while one was open for 1% of the time, Pallas kernels for 0%

commit v1 on v0

--- a/solution.py
+++ b/solution.py
@@ -4,20 +4,50 @@
 from jax.sharding import PartitionSpec as P
 
 LEV = 5
+ROWS = 16
+RING = [[0, 2, 4, 6], [1, 3, 5, 7]]
+TWIN = [(i, i ^ 1) for i in range(8)]
 
 
 def block_start(tree_depth):
     return (tree_depth - 2) * 2**tree_depth + 2
 
 
+def one_shot_ring(values):
+    copies = jnp.broadcast_to(values[None], (4,) + values.shape)
+    parts = lax.all_to_all(copies, "pcol", 0, 0, axis_index_groups=RING)
+    return parts.sum(axis=0)
+
+
 def sum_columns(values):
-    result = lax.psum(values, "pcol")
-    return lax.optimization_barrier(result)
+    shape = values.shape
+    flat = values.reshape(shape[0] * shape[1], shape[2])
+    if shape[0] <= 2:
+        flat = flat + lax.ppermute(flat, "pcol", TWIN)
+        return lax.optimization_barrier(one_shot_ring(flat).reshape(shape))
+    halves = flat.reshape(2, -1, shape[2])
+    core = lax.axis_index("pcol") % 2
+    mine = lax.dynamic_index_in_dim(halves, core, 0, keepdims=False)
+    other = lax.dynamic_index_in_dim(halves, 1 - core, 0, keepdims=False)
+    mine = mine + lax.ppermute(other, "pcol", TWIN)
+    mine = one_shot_ring(mine)
+    other = lax.ppermute(mine, "pcol", TWIN)
+    both = jnp.where(core == 0, jnp.stack([mine, other]), jnp.stack([other, mine]))
+    return lax.optimization_barrier(both.reshape(shape))
 
 
 def sum_rows(values):
-    result = lax.psum(values, "prow")
-    return lax.optimization_barrier(result)
+    shape = values.shape
+    if shape[0] == 1:
+        chunks = values.reshape(8, 8, 2, 128).transpose(0, 2, 1, 3).reshape(ROWS, 8, 128)
+    else:
+        chunks = values.reshape(ROWS, -1, shape[2])
+    part = lax.all_to_all(chunks, "prow", 0, 0).sum(axis=0)
+    copies = jnp.broadcast_to(part[None], chunks.shape)
+    whole = lax.all_to_all(copies, "prow", 0, 0)
+    if shape[0] == 1:
+        whole = whole.reshape(8, 2, 8, 128).transpose(0, 2, 1, 3)
+    return lax.optimization_barrier(whole.reshape(shape))
 
 
 def per_device(rhs, factor, inverse, pattern):

time: 1300 us -> 436 us (0.34)
  waiting for transfers between devices: 1170 us -> 70.8 us
  blocking collectives: 45.5 us -> 239 us
  starting transfers between devices: 0.67 us -> 64.4 us
  between operations: 14.3 us -> 1.29 us
    psum x16 -> x0, waiting for transfers between devices: 1170 us -> none  [the longest x9 759 us: sum_rows(): result = lax.psum(values, 'prow')]
    all_to_all x0 -> x20, blocking collectives: none -> 239 us  [the longest x8 110 us: sum_rows(): part = lax.all_to_all(chunks, 'prow', 0, 0).sum(axis=0)]
    all_to_all x0 -> x7, waiting for transfers between devices: none -> 58.5 us  [the longest x4 35.7 us: sum_rows(): whole = lax.all_to_all(copies, 'prow', 0, 0)]
    psum x2 -> x0, blocking collectives: 45.5 us -> none  [sum_columns(): result = lax.psum(values, 'pcol')]
    ppermute x0 -> x14, starting transfers between devices: none -> 39.3 us  [the longest x5 17.2 us: sum_columns(): mine = mine + lax.ppermute(other, 'pcol', TWIN)]
    all_to_all x0 -> x7, starting transfers between devices: none -> 25.1 us  [the longest x4 14.8 us: sum_rows(): whole = lax.all_to_all(copies, 'prow', 0, 0)]
  transfers between devices with their start and end apart: 16 -> 21, of which waited for: 16 -> 20; matrix products, arithmetic and copies ran while one was open for 1% -> 2% of each run, Pallas kernels for 0% -> 0%
where the time goes in v1:
time: 436 us; the launch traced here: 433 us
  blocking collectives  239 us (55%)
  waiting for transfers between devices  70.8 us (16%)
  starting transfers between devices  64.4 us (15%)
  matrix products  40.8 us (9%)
  local copies, waits for them, and re-layouts  12.7 us (3%)
    all_to_all x8, blocking collectives, sum_rows(): part = lax.all_to_all(chunks, 'prow', 0, 0).sum(axis=0)  110 us
    all_to_all x7, blocking collectives, one_shot_ring(): parts = lax.all_to_all(copies, 'pcol', 0, 0, axis_index_groups=RING)  66.8 us
    all_to_all x5, blocking collectives, sum_rows(): whole = lax.all_to_all(copies, 'prow', 0, 0)  61.7 us
    all_to_all x4, waiting for transfers between devices, sum_rows(): whole = lax.all_to_all(copies, 'prow', 0, 0)  35.7 us
    all_to_all x2, waiting for transfers between devices, one_shot_ring(): parts = lax.all_to_all(copies, 'pcol', 0, 0, axis_index_groups=RING)  17.6 us
    ppermute x5, starting transfers between devices, sum_columns(): mine = mine + lax.ppermute(other, 'pcol', TWIN)  17.2 us
    ppermute x4, starting transfers between devices, sum_columns(): flat = flat + lax.ppermute(flat, 'pcol', TWIN)  14.9 us
    all_to_all x4, starting transfers between devices, sum_rows(): whole = lax.all_to_all(copies, 'prow', 0, 0)  14.8 us
  transfers between devices with their start and end apart: 21, of which 20 were waited for; matrix products, arithmetic and copies ran while one was open for 2% of the time, Pallas kernels for 0%

profile of v1, /device:TPU:1, one launch (start us, length us, event | category | flops | bytes accessed | tf_op | source)
XLA Modules:
  0.0 433.0 jit_solution(12904931937092493780)
XLA Ops:
  0.6 1.9 fusion.20
  2.5 24.1 %all_to_all.135 = f32[16,64,256]{2,1,0:T(8,128)S(1)} all-to-all(f32[16,64,256]{2,1,0:T(8,128)S(1)} %fusion.20), channel_id=1, replica_groups=mesh['prow'=16,'pcol'=8] {'prow'}, dimensions={0} | all-to-all | bytes 2097152 | tf_op jit(solution)/shard_map/all_to_all | solution.py:45
  27.8 3.7 all-to-all-start.1
  31.8 14.3 %all-to-all-done.1 = f32[16,64,256]{2,1,0:T(8,128)S(1)} async-done(((f32[16,64,256]{2,1,0:T(8,128)}), f32[16,64,256]{2,1,0:T(8,128)S(1)}, u32[]{:S(2)}, u32[]{:S(2)}) %all-to-all-start.1) | async-done | bytes 1048608 | tf_op jit(solution)/shard_map/all_to_all | solution.py:47
  46.2 1.7 bitcast_reduce_fusion.2
  48.1 1.7 bitcast_reduce_fusion.1
  49.8 1.7 bitcast_reduce_fusion
  51.5 1.7 fusion.5
  53.3 3.4 collective-permute-start
  57.8 12.6 %all_to_all.136 = f32[4,256,128]{2,1,0:T(8,128)S(1)} all-to-all(f32[4,256,128]{2,1,0:T(8,128)S(1)} %broadcast_in_dim.49), channel_id=1, replica_groups={{0,2,4,6},{1,3,5,7},{8,10,12,14},{9,11,13,15},{16,18,20,22},{17,19,21,2..., dimensions={0} | all-to-all | bytes 1048576 | tf_op jit(solution)/shard_map/all_to_all | solution.py:18
  70.4 1.9 collective-permute-start.1
  73.3 1.4 fusion.31
  74.7 13.5 %all_to_all.137 = f32[16,32,256]{2,1,0:T(8,128)S(1)} all-to-all(f32[16,32,256]{2,1,0:T(8,128)S(1)} %bitcast.138), channel_id=1, replica_groups=mesh['prow'=16,'pcol'=8] {'prow'}, dimensions={0} | all-to-all | bytes 1048576 | tf_op jit(solution)/shard_map/all_to_all | solution.py:45
  89.1 3.7 all-to-all-start.4
  93.2 8.9 %all-to-all-done.4 = f32[16,32,256]{2,1,0:T(8,128)S(1)} async-done(((f32[16,32,256]{2,1,0:T(8,128)}), f32[16,32,256]{2,1,0:T(8,128)S(1)}, u32[]{:S(2)}, u32[]{:S(2)}) %all-to-all-start.4) | async-done | bytes 524320 | tf_op jit(solution)/shard_map/all_to_all | solution.py:47
  102.1 1.3 bitcast_reduce_fusion.4
  103.5 1.4 bitcast_reduce_fusion.3
  105.9 3.3 collective-permute-start.2
  110.2 8.8 %all_to_all.138 = f32[4,128,128]{2,1,0:T(8,128)S(1)} all-to-all(f32[4,128,128]{2,1,0:T(8,128)S(1)} %broadcast_in_dim.51), channel_id=1, replica_groups={{0,2,4,6},{1,3,5,7},{8,10,12,14},{9,11,13,15},{16,18,20,22},{17,19,21,2..., dimensions={0} | all-to-all | bytes 524288 | tf_op jit(solution)/shard_map/all_to_all | solution.py:18
  122.4 10.5 %all_to_all.139 = f32[16,16,256]{2,1,0:T(8,128)S(1)} all-to-all(f32[16,16,256]{2,1,0:T(8,128)S(1)} %bitcast.150), channel_id=1, replica_groups=mesh['prow'=16,'pcol'=8] {'prow'}, dimensions={0} | all-to-all | bytes 524288 | tf_op jit(solution)/shard_map/all_to_all | solution.py:45
  133.7 3.7 all-to-all-start.7
  137.8 7.0 %all-to-all-done.7 = f32[16,16,256]{2,1,0:T(8,128)S(1)} async-done(((f32[16,16,256]{2,1,0:T(8,128)}), f32[16,16,256]{2,1,0:T(8,128)S(1)}, u32[]{:S(2)}, u32[]{:S(2)}) %all-to-all-start.7) | async-done | bytes 262176 | tf_op jit(solution)/shard_map/all_to_all | solution.py:47
  146.0 3.0 collective-permute-start.4
  149.9 8.8 %all_to_all.140 = f32[4,128,128]{2,1,0:T(8,128)S(1)} all-to-all(f32[4,128,128]{2,1,0:T(8,128)S(1)} %broadcast_in_dim.53), channel_id=1, replica_groups={{0,2,4,6},{1,3,5,7},{8,10,12,14},{9,11,13,15},{16,18,20,22},{17,19,21,2..., dimensions={0} | all-to-all | bytes 524288 | tf_op jit(solution)/shard_map/all_to_all | solution.py:18
  158.8 1.8 fusion.57
  160.6 3.5 all-to-all-start.9
  164.1 1.3 fusion.7
  165.4 5.3 %all-to-all-done.9 = f32[16,8,256]{2,1,0:T(8,128)S(1)} async-done(((f32[16,8,256]{2,1,0:T(8,128)}), f32[16,8,256]{2,1,0:T(8,128)S(1)}, u32[]{:S(2)}, u32[]{:S(2)}) %all-to-all-start.9) | async-done | bytes 131104 | tf_op jit(solution)/shard_map/all_to_all | solution.py:45
  171.4 3.6 all-to-all-start.10
  176.2 5.5 %all-to-all-done.10 = f32[16,8,256]{2,1,0:T(8,128)S(1)} async-done(((f32[16,8,256]{2,1,0:T(8,128)}), f32[16,8,256]{2,1,0:T(8,128)S(1)}, u32[]{:S(2)}, u32[]{:S(2)}) %all-to-all-start.10) | async-done | bytes 131104 | tf_op jit(solution)/shard_map/all_to_all | solution.py:47
  183.6 3.7 collective-permute-start.5
  188.9 3.3 all-to-all-start.11
  192.2 4.8 %all-to-all-done.11 = f32[4,64,128]{2,1,0:T(8,128)S(1)} async-done(((f32[4,64,128]{2,1,0:T(8,128)}), f32[4,64,128]{2,1,0:T(8,128)S(1)}, u32[]{:S(2)}, u32[]{:S(2)}) %all-to-all-start.11) | async-done | bytes 131104 | tf_op jit(solution)/shard_map/all_to_all | solution.py:18
  197.9 9.6 %all_to_all.141 = f32[16,8,128]{2,1,0:T(8,128)S(1)} all-to-all(f32[16,8,128]{2,1,0:T(8,128)S(1)} %bitcast.174), channel_id=1, replica_groups=mesh['prow'=16,'pcol'=8] {'prow'}, dimensions={0} | all-to-all | bytes 131072 | tf_op jit(solution)/shard_map/all_to_all | solution.py:45
  207.6 9.8 %all_to_all.142 = f32[16,8,128]{2,1,0:T(8,128)S(1)} all-to-all(f32[16,8,128]{2,1,0:T(8,128)S(1)} %broadcast_in_dim.56), channel_id=1, replica_groups=mesh['prow'=16,'pcol'=8] {'prow'}, dimensions={0} | all-to-all | bytes 131072 | tf_op jit(solution)/shard_map/all_to_all | solution.py:47
  218.3 4.1 collective-permute-start.6
  223.2 7.2 %all_to_all.143 = f32[4,64,128]{2,1,0:T(8,128)S(1)} all-to-all(f32[4,64,128]{2,1,0:T(8,128)S(1)} %broadcast_in_dim.57), channel_id=1, replica_groups={{0,2,4,6},{1,3,5,7},{8,10,12,14},{9,11,13,15},{16,18,20,22},{17,19,21,2..., dimensions={0} | all-to-all | bytes 262144 | tf_op jit(solution)/shard_map/all_to_all | solution.py:18
  232.2 9.7 %all_to_all.144 = f32[16,8,256]{2,1,0:T(8,128)S(1)} all-to-all(f32[16,8,256]{2,1,0:T(8,128)S(1)} %bitcast.170), channel_id=1, replica_groups=mesh['prow'=16,'pcol'=8] {'prow'}, dimensions={0} | all-to-all | bytes 262144 | tf_op jit(solution)/shard_map/all_to_all | solution.py:45
  241.9 10.0 %all_to_all.145 = f32[16,8,256]{2,1,0:T(8,128)S(1)} all-to-all(f32[16,8,256]{2,1,0:T(8,128)S(1)} %broadcast_in_dim.58), channel_id=1, replica_groups=mesh['prow'=16,'pcol'=8] {'prow'}, dimensions={0} | all-to-all | bytes 262144 | tf_op jit(solution)/shard_map/all_to_all | solution.py:47
  253.0 4.1 collective-permute-start.7
  258.1 8.8 %all_to_all.146 = f32[4,128,128]{2,1,0:T(8,128)S(1)} all-to-all(f32[4,128,128]{2,1,0:T(8,128)S(1)} %broadcast_in_dim.59), channel_id=1, replica_groups={{0,2,4,6},{1,3,5,7},{8,10,12,14},{9,11,13,15},{16,18,20,22},{17,19,21,2..., dimensions={0} | all-to-all | bytes 524288 | tf_op jit(solution)/shard_map/all_to_all | solution.py:18
  269.8 10.4 %all_to_all.147 = f32[16,16,256]{2,1,0:T(8,128)S(1)} all-to-all(f32[16,16,256]{2,1,0:T(8,128)S(1)} %bitcast.157), channel_id=1, replica_groups=mesh['prow'=16,'pcol'=8] {'prow'}, dimensions={0} | all-to-all | bytes 524288 | tf_op jit(solution)/shard_map/all_to_all | solution.py:45
  280.3 10.8 %all_to_all.148 = f32[16,16,256]{2,1,0:T(8,128)S(1)} all-to-all(f32[16,16,256]{2,1,0:T(8,128)S(1)} %broadcast_in_dim.61), channel_id=1, replica_groups=mesh['prow'=16,'pcol'=8] {'prow'}, dimensions={0} | all-to-all | bytes 524288 | tf_op jit(solution)/shard_map/all_to_all | solution.py:47
  292.3 3.8 collective-permute-start.8
  297.1 8.8 %all_to_all.149 = f32[4,128,128]{2,1,0:T(8,128)S(1)} all-to-all(f32[4,128,128]{2,1,0:T(8,128)S(1)} %broadcast_in_dim.62), channel_id=1, replica_groups={{0,2,4,6},{1,3,5,7},{8,10,12,14},{9,11,13,15},{16,18,20,22},{17,19,21,2..., dimensions={0} | all-to-all | bytes 524288 | tf_op jit(solution)/shard_map/all_to_all | solution.py:18
  305.9 1.4 collective-permute-start.9
  310.3 1.3 fusion.4
  311.6 1.3 fusion.3
  312.8 13.6 %all_to_all.150 = f32[16,32,256]{2,1,0:T(8,128)S(1)} all-to-all(f32[16,32,256]{2,1,0:T(8,128)S(1)} %bitcast.144), channel_id=1, replica_groups=mesh['prow'=16,'pcol'=8] {'prow'}, dimensions={0} | all-to-all | bytes 1048576 | tf_op jit(solution)/shard_map/all_to_all | solution.py:45
  326.5 12.7 %all_to_all.151 = f32[16,32,256]{2,1,0:T(8,128)S(1)} all-to-all(f32[16,32,256]{2,1,0:T(8,128)S(1)} %broadcast_in_dim.65), channel_id=1, replica_groups=mesh['prow'=16,'pcol'=8] {'prow'}, dimensions={0} | all-to-all | bytes 1048576 | tf_op jit(solution)/shard_map/all_to_all | solution.py:47
  340.5 3.3 collective-permute-start.10
  344.9 11.6 %all_to_all.152 = f32[4,256,128]{2,1,0:T(8,128)S(1)} all-to-all(f32[4,256,128]{2,1,0:T(8,128)S(1)} %broadcast_in_dim.66), channel_id=1, replica_groups={{0,2,4,6},{1,3,5,7},{8,10,12,14},{9,11,13,15},{16,18,20,22},{17,19,21,2..., dimensions={0} | all-to-all | bytes 1048576 | tf_op jit(solution)/shard_map/all_to_all | solution.py:18
  356.6 1.3 collective-permute-start.11
  359.6 1.5 convolution_multiply_fusion.3
  361.2 1.5 fusion.2
  362.8 1.5 fusion.1
  364.4 1.5 fusion
  365.9 18.9 %all_to_all.153 = f32[16,64,256]{2,1,0:T(8,128)S(1)} all-to-all(f32[16,64,256]{2,1,0:T(8,128)S(1)} %fusion), channel_id=1, replica_groups=mesh['prow'=16,'pcol'=8] {'prow'}, dimensions={0} | all-to-all | bytes 2097152 | tf_op jit(solution)/shard_map/all_to_all | solution.py:45
  385.0 18.3 %all_to_all.154 = f32[16,64,256]{2,1,0:T(8,128)S(1)} all-to-all(f32[16,64,256]{2,1,0:T(8,128)S(1)} %broadcast_in_dim.70), channel_id=1, replica_groups=mesh['prow'=16,'pcol'=8] {'prow'}, dimensions={0} | all-to-all | bytes 2097152 | tf_op jit(solution)/shard_map/all_to_all | solution.py:47
  403.4 1.6 fusion.18
  405.0 3.3 collective-permute-start.12
  410.6 3.5 all-to-all-start.26
  416.1 12.8 %all-to-all-done.26 = f32[4,512,128]{2,1,0:T(8,128)S(1)} async-done(((f32[4,512,128]{2,1,0:T(8,128)}), f32[4,512,128]{2,1,0:T(8,128)S(1)}, u32[]{:S(2)}, u32[]{:S(2)}) %all-to-all-start.26) | async-done | bytes 1048608 | tf_op jit(solution)/shard_map/all_to_all | solution.py:18
  429.0 1.3 collective-permute-start.13
  (127 shorter events, 45.0 us)
Async XLA Ops:
  0.6 30.8 %copy-start.1 = (s32[98]{0:T(128)S(1)}, s32[98]{0:T(128)}, u32[]{:S(2)}) copy-start(s32[98]{0:T(128)} %param.27) | copy-start | bytes 1180
  27.8 18.4 %all-to-all-start.1 = ((f32[16,64,256]{2,1,0:T(8,128)}), f32[16,64,256]{2,1,0:T(8,128)S(1)}, u32[]{:S(2)}, u32[]{:S(2)}) async-start(f32[16,64,256]{2,1,0:T(8,128)} %broadcast_in_dim.48), calls=%async_computation.1 | async-start | bytes 2097152 | tf_op jit(solution)/shard_map/all_to_all | solution.py:47
  53.3 4.4 %collective-permute-start = (f32[256,128]{1,0:T(8,128)S(1)}, f32[256,128]{1,0:T(8,128)S(1)}, u32[]{:S(2)}, u32[]{:S(2)}) collective-permute-start(f32[256,128]{1,0:T(8,128)S(1)} %dynamic-slice_bitcast_fusion.2), channel_id=1, source_target_pairs={{0,1},{1,0},{2,3},{3,2},{4,5},{5,4},{6,7},{7,6},{8,9},{9,8},{10,11... | collective-permute-start | bytes 393224 | tf_op jit(solution)/shard_map/ppermute | solution.py:32
  70.4 2.9 collective-permute-start.1
  89.1 13.0 %all-to-all-start.4 = ((f32[16,32,256]{2,1,0:T(8,128)}), f32[16,32,256]{2,1,0:T(8,128)S(1)}, u32[]{:S(2)}, u32[]{:S(2)}) async-start(f32[16,32,256]{2,1,0:T(8,128)} %broadcast_in_dim.50), calls=%async_computation.4 | async-start | bytes 1048576 | tf_op jit(solution)/shard_map/all_to_all | solution.py:47
  103.5 93.5 %slice-start = ((bf16[31,256,128]{2,1,0:T(8,128)(2,1)}), bf16[1,256,128]{2,1,0:T(8,128)(2,1)S(1)}, s32[]{:S(2)}) async-start(bf16[31,256,128]{2,1,0:T(8,128)(2,1)} %param.26), calls=%async_computation.27 | async-start | bytes 131072 | tf_op jit(solution)/shard_map/slice | solution.py:67
  104.9 1.0 copy-start
  105.9 4.2 collective-permute-start.2
  119.0 2.2 collective-permute-start.3
  133.7 11.1 %all-to-all-start.7 = ((f32[16,16,256]{2,1,0:T(8,128)}), f32[16,16,256]{2,1,0:T(8,128)S(1)}, u32[]{:S(2)}, u32[]{:S(2)}) async-start(f32[16,16,256]{2,1,0:T(8,128)} %broadcast_in_dim.52), calls=%async_computation.7 | async-start | bytes 524288 | tf_op jit(solution)/shard_map/all_to_all | solution.py:47
  146.0 3.9 collective-permute-start.4
  160.6 10.2 %all-to-all-start.9 = ((f32[16,8,256]{2,1,0:T(8,128)}), f32[16,8,256]{2,1,0:T(8,128)S(1)}, u32[]{:S(2)}, u32[]{:S(2)}) async-start(f32[16,8,256]{2,1,0:T(8,128)} %bitcast.27), calls=%async_computation.9 | async-start | bytes 262144 | tf_op jit(solution)/shard_map/all_to_all | solution.py:45
  171.4 10.3 %all-to-all-start.10 = ((f32[16,8,256]{2,1,0:T(8,128)}), f32[16,8,256]{2,1,0:T(8,128)S(1)}, u32[]{:S(2)}, u32[]{:S(2)}) async-start(f32[16,8,256]{2,1,0:T(8,128)} %broadcast_in_dim.54), calls=%async_computation.10 | async-start | bytes 262144 | tf_op jit(solution)/shard_map/all_to_all | solution.py:47
  183.6 4.6 %collective-permute-start.5 = (f32[64,128]{1,0:T(8,128)S(1)}, f32[64,128]{1,0:T(8,128)S(1)}, u32[]{:S(2)}, u32[]{:S(2)}) collective-permute-start(f32[64,128]{1,0:T(8,128)S(1)} %fusion.70), channel_id=1, source_target_pairs={{0,1},{1,0},{2,3},{3,2},{4,5},{5,4},{6,7},{7,6},{8,9},{9,8},{10,11... | collective-permute-start | bytes 98312 | tf_op jit(solution)/shard_map/ppermute | solution.py:26
  188.9 8.1 %all-to-all-start.11 = ((f32[4,64,128]{2,1,0:T(8,128)}), f32[4,64,128]{2,1,0:T(8,128)S(1)}, u32[]{:S(2)}, u32[]{:S(2)}) async-start(f32[4,64,128]{2,1,0:T(8,128)} %broadcast_in_dim.55), calls=%async_computation.11 | async-start | bytes 262144 | tf_op jit(solution)/shard_map/all_to_all | solution.py:18
  218.3 4.9 %collective-permute-start.6 = (f32[64,128]{1,0:T(8,128)S(1)}, f32[64,128]{1,0:T(8,128)S(1)}, u32[]{:S(2)}, u32[]{:S(2)}) collective-permute-start(f32[64,128]{1,0:T(8,128)S(1)} %fusion.60), channel_id=1, source_target_pairs={{0,1},{1,0},{2,3},{3,2},{4,5},{5,4},{6,7},{7,6},{8,9},{9,8},{10,11... | collective-permute-start | bytes 98312 | tf_op jit(solution)/shard_map/ppermute | solution.py:26
  253.0 5.0 %collective-permute-start.7 = (f32[128,128]{1,0:T(8,128)S(1)}, f32[128,128]{1,0:T(8,128)S(1)}, u32[]{:S(2)}, u32[]{:S(2)}) collective-permute-start(f32[128,128]{1,0:T(8,128)S(1)} %bitcast.172), channel_id=1, source_target_pairs={{0,1},{1,0},{2,3},{3,2},{4,5},{5,4},{6,7},{7,6},{8,9},{9,8},{10,11... | collective-permute-start | bytes 196616 | tf_op jit(solution)/shard_map/ppermute | solution.py:26
  292.3 4.7 %collective-permute-start.8 = (f32[128,128]{1,0:T(8,128)S(1)}, f32[128,128]{1,0:T(8,128)S(1)}, u32[]{:S(2)}, u32[]{:S(2)}) collective-permute-start(f32[128,128]{1,0:T(8,128)S(1)} %dynamic-slice_bitcast_fusion.3), channel_id=1, source_target_pairs={{0,1},{1,0},{2,3},{3,2},{4,5},{5,4},{6,7},{7,6},{8,9},{9,8},{10,11... | collective-permute-start | bytes 196616 | tf_op jit(solution)/shard_map/ppermute | solution.py:32
  305.9 2.3 collective-permute-start.9
  340.5 4.3 %collective-permute-start.10 = (f32[256,128]{1,0:T(8,128)S(1)}, f32[256,128]{1,0:T(8,128)S(1)}, u32[]{:S(2)}, u32[]{:S(2)}) collective-permute-start(f32[256,128]{1,0:T(8,128)S(1)} %dynamic-slice_bitcast_fusion.1), channel_id=1, source_target_pairs={{0,1},{1,0},{2,3},{3,2},{4,5},{5,4},{6,7},{7,6},{8,9},{9,8},{10,11... | collective-permute-start | bytes 393224 | tf_op jit(solution)/shard_map/ppermute | solution.py:32
  356.6 2.3 collective-permute-start.11
  405.0 4.5 %collective-permute-start.12 = (f32[512,128]{1,0:T(8,128)S(1)}, f32[512,128]{1,0:T(8,128)S(1)}, u32[]{:S(2)}, u32[]{:S(2)}) collective-permute-start(f32[512,128]{1,0:T(8,128)S(1)} %dynamic-slice_bitcast_fusion), channel_id=1, source_target_pairs={{0,1},{1,0},{2,3},{3,2},{4,5},{5,4},{6,7},{7,6},{8,9},{9,8},{10,11... | collective-permute-start | bytes 786440 | tf_op jit(solution)/shard_map/ppermute | solution.py:32
  410.6 18.3 %all-to-all-start.26 = ((f32[4,512,128]{2,1,0:T(8,128)}), f32[4,512,128]{2,1,0:T(8,128)S(1)}, u32[]{:S(2)}, u32[]{:S(2)}) async-start(f32[4,512,128]{2,1,0:T(8,128)} %broadcast_in_dim.71), calls=%async_computation.26 | async-start | bytes 2097152 | tf_op jit(solution)/shard_map/all_to_all | solution.py:18
  429.0 3.2 collective-permute-start.13

commit v2 on v1

v2 whole, which is shorter than its diff:
```python
import jax
import jax.numpy as jnp
from jax import lax
from jax.sharding import PartitionSpec as P

LEV = 5
ROWS = 16
RING = [[0, 2, 4, 6], [1, 3, 5, 7]]
TWIN = [(i, i ^ 1) for i in range(8)]


def block_start(tree_depth):
    return (tree_depth - 2) * 2**tree_depth + 2


def blocks_of(array, tree_depth, upward):
    start = block_start(tree_depth)
    count = 2**tree_depth
    return array[start + upward - 1 : start + count * tree_depth : tree_depth]


def product(left, right, form):
    return jnp.einsum(form, left, right, preferred_element_type=jnp.float32)


def one_shot_ring(values):
    copies = jnp.broadcast_to(values[None], (4,) + values.shape)
    parts = lax.all_to_all(copies, "pcol", 0, 0, axis_index_groups=RING)
    return parts.sum(axis=0)


def sum_columns(values):
    shape = values.shape
    flat = values.reshape(-1, shape[-1])
    if flat.shape[0] <= 128:
        flat = flat + lax.ppermute(flat, "pcol", TWIN)
        return one_shot_ring(flat).reshape(shape)
    halves = flat.reshape(2, -1, shape[-1])
    core = lax.axis_index("pcol") % 2
    mine = lax.dynamic_index_in_dim(halves, core, 0, keepdims=False)
    other = lax.dynamic_index_in_dim(halves, 1 - core, 0, keepdims=False)
    mine = mine + lax.ppermute(other, "pcol", TWIN)
    mine = one_shot_ring(mine)
    other = lax.ppermute(mine, "pcol", TWIN)
    both = jnp.where(core == 0, jnp.stack([mine, other]), jnp.stack([other, mine]))
    return both.reshape(shape)


def sum_rows(values):
    shape = values.shape
    chunks = values.reshape(ROWS, -1, shape[-1])
    part = lax.all_to_all(chunks, "prow", 0, 0).sum(axis=0)
    copies = jnp.broadcast_to(part[None], chunks.shape)
    whole = lax.all_to_all(copies, "prow", 0, 0)
    return whole.reshape(shape)


def per_device(rhs, factor, inverse, pattern):
    live = pattern.astype(jnp.float32)
    bf16 = jnp.bfloat16
    halves = factor[0:2].reshape(2, 128, 2, 128).transpose(0, 2, 1, 3).reshape(2, 256, 128)
    top = jnp.concatenate([inverse[0:1], halves]).astype(jnp.float32)
    scale = jnp.concatenate([jnp.ones((1,), jnp.float32), live[0:2]])
    top = (lax.all_gather(top, "prow") * scale[:, None, None]).astype(bf16)
    inverse_top = top[:, 0]
    factor_top = top[:, 1:].reshape(ROWS, 2, 2, 128, 128)

    partial_value = [[] for _ in range(LEV)]
    forward_levels = [None] * LEV

    def push_up(narrow, tree_depth):
        count = 2**tree_depth
        for upward in range(1, tree_depth + 1):
            terms = product(narrow, blocks_of(factor, tree_depth, upward), "nrc,nwc->nrw")
            terms = terms * blocks_of(live, tree_depth, upward)[:, None, None]
            groups = count >> upward
            terms = terms.reshape((groups, 2**upward) + terms.shape[1:]).sum(axis=1)
            partial_value[tree_depth - upward].append(terms)

    for tree_depth in range(LEV - 1, 0, -1):
        first = 2**tree_depth - 1
        count = 2**tree_depth
        residual = rhs[first : first + count]
        if tree_depth < LEV - 1:
            residual = residual - sum_columns(sum(partial_value[tree_depth]))
        pieces = product(residual.astype(bf16), inverse[first : first + count], "nrc,nwc->nrw")
        if tree_depth > 1:
            forward_levels[tree_depth] = sum_rows(pieces)
            push_up(forward_levels[tree_depth].astype(bf16), tree_depth)

    here = (lax.axis_index("pcol") == 0).astype(jnp.float32)
    root_part = sum(partial_value[0])[0] - rhs[0] * here
    sent = jnp.concatenate([pieces[0], pieces[1], root_part], axis=1).reshape(ROWS, 4, 640)
    got = lax.all_to_all(sent, "prow", 0, 0)
    forward_1 = got[:, :, :512].sum(axis=0)
    root_part = got[:, :, 512:]
    for child in range(2):
        narrow = forward_1[:, 256 * child : 256 * child + 256].astype(bf16).reshape(4, 2, 128)
        root_part = root_part + product(narrow, factor_top[:, child], "rhc,phwc->prw")
    residual = -sum_columns(root_part)
    forward_0 = product(residual.astype(bf16), inverse_top, "prc,pwc->prw").sum(axis=0)
    solution_0 = sum_columns(product(forward_0.astype(bf16), inverse_top, "rw,pwc->prc"))
    narrow = solution_0.astype(bf16)
    target_1 = [
        forward_1[:, 256 * child : 256 * child + 256]
        - product(narrow, factor_top[:, child], "prw,phwc->prhc").sum(axis=0).reshape(4, 256)
        for child in range(2)
    ]
    same = jnp.concatenate(target_1 + [forward_1, forward_0], axis=1)
    sent = jnp.concatenate([jnp.broadcast_to(same[None], (ROWS, 4, 1280)), solution_0], axis=2)
    got = lax.all_to_all(sent, "prow", 0, 0).reshape(64, 1408)
    target_1 = jnp.stack([got[:, 0:256], got[:, 256:512]])
    forward_levels[1] = jnp.stack([got[:, 512:768], got[:, 768:1024]])
    forward_levels[0] = got[None, :, 1024:1280]

    gathered = [[] for _ in range(LEV)]

    def push_down(narrow, tree_depth):
        for lower in range(max(tree_depth + 1, 2), LEV):
            upward = lower - tree_depth
            above = jnp.repeat(narrow, 2**upward, axis=0)
            terms = product(above, blocks_of(factor, lower, upward), "nrw,nwc->nrc")
            gathered[lower].append(terms * blocks_of(live, lower, upward)[:, None, None])

    solved = [got[None, :, 1280:1408]] + [None] * (LEV - 1)
    push_down(solved[0].astype(bf16), 0)
    for tree_depth in range(1, LEV):
        first = 2**tree_depth - 1
        count = 2**tree_depth
        if tree_depth == 1:
            target_vec = target_1
        else:
            target_vec = forward_levels[tree_depth] - sum_rows(sum(gathered[tree_depth]))
        pieces = product(target_vec.astype(bf16), inverse[first : first + count], "nrw,nwc->nrc")
        solved[tree_depth] = sum_columns(pieces)
        push_down(solved[tree_depth].astype(bf16), tree_depth)
    return (jnp.concatenate(solved, axis=0), jnp.concatenate(forward_levels, axis=0))


def solution(mesh):
    in_specs = (P(None, None, "prow"), P(None, "prow", "pcol"), P(None, "pcol", "prow"), P())
    out_specs = (P(None, None, "prow"), P(None, None, "pcol"))
    return jax.shard_map(
        per_device, mesh=mesh, in_specs=in_specs, out_specs=out_specs, check_vma=False
    )
```

time: 436 us -> 428 us (0.982)
  blocking collectives: 239 us -> 139 us
  starting transfers between devices: 64.4 us -> 95.4 us
  waiting for transfers between devices: 70.8 us -> 98.3 us
  between operations: 1.29 us -> 15 us
  local copies, waits for them, and re-layouts: 12.7 us -> 24.1 us
  other arithmetic: 4.33 us -> 10.9 us
    all_to_all x7 -> x2, blocking collectives: 66.8 us -> 20.4 us  [one_shot_ring(): parts = lax.all_to_all(copies, 'pcol', 0, 0, axis_index_groups=RING)]
    all_to_all x8 -> x4, blocking collectives: 110 us -> 75.7 us  [sum_rows(): part = lax.all_to_all(chunks, 'prow', 0, 0).sum(axis=0)]
    all_to_all x5 -> x2, blocking collectives: 61.7 us -> 32.1 us  [sum_rows(): whole = lax.all_to_all(copies, 'prow', 0, 0)]
    all_to_all x2 -> x7, waiting for transfers between devices: 17.6 us -> 42.1 us  [one_shot_ring(): parts = lax.all_to_all(copies, 'pcol', 0, 0, axis_index_groups=RING)]
    all_to_all x2 -> x7, starting transfers between devices: 6.84 us -> 24.9 us  [one_shot_ring(): parts = lax.all_to_all(copies, 'pcol', 0, 0, axis_index_groups=RING)]
    all_to_all x0 -> x1, blocking collectives: none -> 11 us  [per_device(): got = lax.all_to_all(sent, 'prow', 0, 0).reshape(64, 1408)]
    ppermute x5, starting transfers between devices: 17.2 us -> 27.2 us  [sum_columns(): mine = mine + lax.ppermute(other, 'pcol', TWIN)]
    all_to_all x0 -> x1, waiting for transfers between devices: none -> 6.82 us  [per_device(): got = lax.all_to_all(sent, 'prow', 0, 0)]
  transfers between devices with their start and end apart: 21 -> 29, of which waited for: 20 -> 23; matrix products, arithmetic and copies ran while one was open for 2% -> 11% of each run, Pallas kernels for 0% -> 0%
where the time goes in v2:
time: 428 us; the launch traced here: 425 us
  blocking collectives  139 us (32%)
  waiting for transfers between devices  98.3 us (23%)
  starting transfers between devices  95.4 us (22%)
  matrix products  41.9 us (10%)
  local copies, waits for them, and re-layouts  24.1 us (6%)
  between operations  15 us (4%)
  other arithmetic  10.9 us (3%)
    all_to_all x4, blocking collectives, sum_rows(): part = lax.all_to_all(chunks, 'prow', 0, 0).sum(axis=0)  75.7 us
    all_to_all x7, waiting for transfers between devices, one_shot_ring(): parts = lax.all_to_all(copies, 'pcol', 0, 0, axis_index_groups=RING)  42.1 us
    dot_general x32, matrix products, product(): return jnp.einsum(form, left, right, preferred_element_type=jnp.float32)  41.9 us
    all_to_all x2, blocking collectives, sum_rows(): whole = lax.all_to_all(copies, 'prow', 0, 0)  32.1 us
    all_to_all x4, waiting for transfers between devices, sum_rows(): whole = lax.all_to_all(copies, 'prow', 0, 0)  29.7 us
    ppermute x5, starting transfers between devices, sum_columns(): mine = mine + lax.ppermute(other, 'pcol', TWIN)  27.2 us
    all_to_all x7, starting transfers between devices, one_shot_ring(): parts = lax.all_to_all(copies, 'pcol', 0, 0, axis_index_groups=RING)  24.9 us
    all_to_all x2, blocking collectives, one_shot_ring(): parts = lax.all_to_all(copies, 'pcol', 0, 0, axis_index_groups=RING)  20.4 us
  transfers between devices with their start and end apart: 29, of which 23 were waited for; matrix products, arithmetic and copies ran while one was open for 11% of the time, Pallas kernels for 0%

profile of v2, /device:TPU:1, one launch (start us, length us, event | category | flops | bytes accessed | tf_op | source)
XLA Modules:
  0.0 424.8 jit_solution(7724188902655608779)
XLA Ops:
  9.8 1.9 fusion.28
  11.7 27.1 %all_to_all.115 = f32[16,64,256]{2,1,0:T(8,128)S(1)} all-to-all(f32[16,64,256]{2,1,0:T(8,128)S(1)} %fusion.28), channel_id=1, replica_groups=mesh['prow'=16,'pcol'=8] {'prow'}, dimensions={0} | all-to-all | bytes 2097152 | tf_op jit(solution)/shard_map/all_to_all | solution.py:52
  39.9 4.9 %all-to-all-start.1 = ((f32[16,64,256]{2,1,0:T(8,128)}), f32[16,64,256]{2,1,0:T(8,128)S(1)}, u32[]{:S(2)}, u32[]{:S(2)}) async-start(f32[16,64,256]{2,1,0:T(8,128)} %broadcast_in_dim.48), calls=%async_computation.1 | async-start | bytes 2097152 | tf_op jit(solution)/shard_map/all_to_all | solution.py:54
  45.0 11.6 %all-to-all-done.1 = f32[16,64,256]{2,1,0:T(8,128)S(1)} async-done(((f32[16,64,256]{2,1,0:T(8,128)}), f32[16,64,256]{2,1,0:T(8,128)S(1)}, u32[]{:S(2)}, u32[]{:S(2)}) %all-to-all-start.1) | async-done | bytes 1048608 | tf_op jit(solution)/shard_map/all_to_all | solution.py:54
  56.6 1.7 bitcast_reduce_fusion.1
  58.4 12.5 %collective-permute-start = (f32[256,128]{1,0:T(8,128)S(1)}, f32[256,128]{1,0:T(8,128)S(1)}, u32[]{:S(2)}, u32[]{:S(2)}) collective-permute-start(f32[256,128]{1,0:T(8,128)S(1)} %dynamic-slice_bitcast_fusion.2), channel_id=1, source_target_pairs={{0,1},{1,0},{2,3},{3,2},{4,5},{5,4},{6,7},{7,6},{8,9},{9,8},{10,11... | collective-permute-start | bytes 393224 | tf_op jit(solution)/shard_map/ppermute | solution.py:42
  71.9 13.2 %all_to_all.116 = f32[4,256,128]{2,1,0:T(8,128)S(1)} all-to-all(f32[4,256,128]{2,1,0:T(8,128)S(1)} %broadcast_in_dim.49), channel_id=1, replica_groups={{0,2,4,6},{1,3,5,7},{8,10,12,14},{9,11,13,15},{16,18,20,22},{17,19,21,2..., dimensions={0} | all-to-all | bytes 1048576 | tf_op jit(solution)/shard_map/all_to_all | solution.py:28
  85.1 1.8 collective-permute-start.1
  89.4 16.6 %all_to_all.117 = f32[16,32,256]{2,1,0:T(8,128)S(1)} all-to-all(f32[16,32,256]{2,1,0:T(8,128)S(1)} %bitcast.217), channel_id=1, replica_groups=mesh['prow'=16,'pcol'=8] {'prow'}, dimensions={0} | all-to-all | bytes 1048576 | tf_op jit(solution)/shard_map/all_to_all | solution.py:52
  106.8 3.7 all-to-all-start.4
  110.8 1.7 bitcast_reduce_fusion
  112.5 7.3 %all-to-all-done.4 = f32[16,32,256]{2,1,0:T(8,128)S(1)} async-done(((f32[16,32,256]{2,1,0:T(8,128)}), f32[16,32,256]{2,1,0:T(8,128)S(1)}, u32[]{:S(2)}, u32[]{:S(2)}) %all-to-all-start.4) | async-done | bytes 524320 | tf_op jit(solution)/shard_map/all_to_all | solution.py:54
  119.9 1.5 bitcast_reduce_fusion.3
  121.4 3.3 collective-permute-start.2
  126.3 3.4 all-to-all-start.5
  129.8 6.1 %all-to-all-done.5 = f32[4,128,128]{2,1,0:T(8,128)S(1)} async-done(((f32[4,128,128]{2,1,0:T(8,128)}), f32[4,128,128]{2,1,0:T(8,128)S(1)}, u32[]{:S(2)}, u32[]{:S(2)}) %all-to-all-start.5) | async-done | bytes 262176 | tf_op jit(solution)/shard_map/all_to_all | solution.py:28
  135.9 1.6 collective-permute-start.3
  138.8 1.9 fusion.55
  140.8 3.5 all-to-all-start.6
  144.3 1.7 fusion.5
  146.1 1.7 bitcast_reduce_fusion.2
  147.8 4.4 %all-to-all-done.6 = f32[16,16,256]{2,1,0:T(8,128)S(1)} async-done(((f32[16,16,256]{2,1,0:T(8,128)}), f32[16,16,256]{2,1,0:T(8,128)S(1)}, u32[]{:S(2)}, u32[]{:S(2)}) %all-to-all-start.6) | async-done | bytes 262176 | tf_op jit(solution)/shard_map/all_to_all | solution.py:52
  153.0 3.9 all-to-all-start.7
  159.6 4.8 %all-to-all-done.7 = f32[16,16,256]{2,1,0:T(8,128)S(1)} async-done(((f32[16,16,256]{2,1,0:T(8,128)}), f32[16,16,256]{2,1,0:T(8,128)S(1)}, u32[]{:S(2)}, u32[]{:S(2)}) %all-to-all-start.7) | async-done | bytes 262176 | tf_op jit(solution)/shard_map/all_to_all | solution.py:54
  165.6 2.4 collective-permute-start.4
  169.9 3.4 all-to-all-start.8
  173.3 6.7 %all-to-all-done.8 = f32[4,128,128]{2,1,0:T(8,128)S(1)} async-done(((f32[4,128,128]{2,1,0:T(8,128)}), f32[4,128,128]{2,1,0:T(8,128)S(1)}, u32[]{:S(2)}, u32[]{:S(2)}) %all-to-all-start.8) | async-done | bytes 262176 | tf_op jit(solution)/shard_map/all_to_all | solution.py:28
  182.0 3.5 all-to-all-start.9
  185.6 6.8 %all-to-all-done.9 = f32[16,4,640]{2,1,0:T(4,128)S(1)} async-done(((f32[16,4,640]{2,1,0:T(4,128)}), f32[16,4,640]{2,1,0:T(4,128)S(1)}, u32[]{:S(2)}, u32[]{:S(2)}) %all-to-all-start.9) | async-done | bytes 163872 | tf_op jit(solution)/shard_map/all_to_all | solution.py:94
  193.0 3.6 multiply_convert_fusion
  198.4 2.1 collective-permute-start.5
  201.3 7.2 %all_to_all.118 = f32[4,64,128]{2,1,0:T(8,128)S(1)} all-to-all(f32[4,64,128]{2,1,0:T(8,128)S(1)} %broadcast_in_dim.54), channel_id=1, replica_groups={{0,2,4,6},{1,3,5,7},{8,10,12,14},{9,11,13,15},{16,18,20,22},{17,19,21,2..., dimensions={0} | all-to-all | bytes 262144 | tf_op jit(solution)/shard_map/all_to_all | solution.py:28
  210.0 1.6 convolution_bitcast_fusion.4
  213.0 1.5 collective-permute-start.6
  216.1 3.9 all-to-all-start.11
  221.5 1.6 copy.20
  223.1 1.6 copy.19
  226.8 11.0 %all_to_all.119 = f32[16,4,1408]{2,1,0:T(4,128)S(1)} all-to-all(f32[16,4,1408]{2,1,0:T(4,128)S(1)} %pad_maximum_fusion), channel_id=1, replica_groups=mesh['prow'=16,'pcol'=8] {'prow'}, dimensions={0} | all-to-all | bytes 720896 | tf_op jit(solution)/shard_map/all_to_all | solution.py:111
  239.0 3.0 collective-permute-start.7
  243.6 3.7 all-to-all-start.13
  248.5 4.7 %all-to-all-done.13 = f32[4,128,128]{2,1,0:T(8,128)S(1)} async-done(((f32[4,128,128]{2,1,0:T(8,128)}), f32[4,128,128]{2,1,0:T(8,128)S(1)}, u32[]{:S(2)}, u32[]{:S(2)}) %all-to-all-start.13) | async-done | bytes 262176 | tf_op jit(solution)/shard_map/all_to_all | solution.py:28
  253.2 1.8 fusion.6
  255.1 3.7 all-to-all-start.14
  259.4 6.7 %all-to-all-done.14 = f32[16,16,256]{2,1,0:T(8,128)S(1)} async-done(((f32[16,16,256]{2,1,0:T(8,128)}), f32[16,16,256]{2,1,0:T(8,128)S(1)}, u32[]{:S(2)}, u32[]{:S(2)}) %all-to-all-start.14) | async-done | bytes 262176 | tf_op jit(solution)/shard_map/all_to_all | solution.py:52
  266.8 3.7 all-to-all-start.15
  271.8 6.0 %all-to-all-done.15 = f32[16,16,256]{2,1,0:T(8,128)S(1)} async-done(((f32[16,16,256]{2,1,0:T(8,128)}), f32[16,16,256]{2,1,0:T(8,128)S(1)}, u32[]{:S(2)}, u32[]{:S(2)}) %all-to-all-start.15) | async-done | bytes 262176 | tf_op jit(solution)/shard_map/all_to_all | solution.py:54
  279.7 4.4 %collective-permute-start.8 = (f32[128,128]{1,0:T(8,128)S(1)}, f32[128,128]{1,0:T(8,128)S(1)}, u32[]{:S(2)}, u32[]{:S(2)}) collective-permute-start(f32[128,128]{1,0:T(8,128)S(1)} %dynamic-slice_bitcast_fusion.3), channel_id=1, source_target_pairs={{0,1},{1,0},{2,3},{3,2},{4,5},{5,4},{6,7},{7,6},{8,9},{9,8},{10,11... | collective-permute-start | bytes 196616 | tf_op jit(solution)/shard_map/ppermute | solution.py:42
  285.7 3.4 all-to-all-start.16
  290.4 4.8 %all-to-all-done.16 = f32[4,128,128]{2,1,0:T(8,128)S(1)} async-done(((f32[4,128,128]{2,1,0:T(8,128)}), f32[4,128,128]{2,1,0:T(8,128)S(1)}, u32[]{:S(2)}, u32[]{:S(2)}) %all-to-all-start.16) | async-done | bytes 262176 | tf_op jit(solution)/shard_map/all_to_all | solution.py:28
  295.2 1.6 collective-permute-start.9
  299.5 13.3 %all_to_all.120 = f32[16,32,256]{2,1,0:T(8,128)S(1)} all-to-all(f32[16,32,256]{2,1,0:T(8,128)S(1)} %bitcast.219), channel_id=1, replica_groups=mesh['prow'=16,'pcol'=8] {'prow'}, dimensions={0} | all-to-all | bytes 1048576 | tf_op jit(solution)/shard_map/all_to_all | solution.py:52
  312.9 13.2 %all_to_all.121 = f32[16,32,256]{2,1,0:T(8,128)S(1)} all-to-all(f32[16,32,256]{2,1,0:T(8,128)S(1)} %broadcast_in_dim.64), channel_id=1, replica_groups=mesh['prow'=16,'pcol'=8] {'prow'}, dimensions={0} | all-to-all | bytes 1048576 | tf_op jit(solution)/shard_map/all_to_all | solution.py:54
  328.3 3.5 collective-permute-start.10
  333.6 3.5 all-to-all-start.19
  337.1 1.5 convolution_multiply_fusion.3
  338.7 1.5 fusion.2
  340.3 6.0 %all-to-all-done.19 = f32[4,256,128]{2,1,0:T(8,128)S(1)} async-done(((f32[4,256,128]{2,1,0:T(8,128)}), f32[4,256,128]{2,1,0:T(8,128)S(1)}, u32[]{:S(2)}, u32[]{:S(2)}) %all-to-all-start.19) | async-done | bytes 524320 | tf_op jit(solution)/shard_map/all_to_all | solution.py:28
  347.7 1.5 fusion.1
  349.4 1.5 fusion
  350.9 18.7 %all_to_all.122 = f32[16,64,256]{2,1,0:T(8,128)S(1)} all-to-all(f32[16,64,256]{2,1,0:T(8,128)S(1)} %fusion), channel_id=1, replica_groups=mesh['prow'=16,'pcol'=8] {'prow'}, dimensions={0} | all-to-all | bytes 2097152 | tf_op jit(solution)/shard_map/all_to_all | solution.py:52
  369.8 18.9 %all_to_all.123 = f32[16,64,256]{2,1,0:T(8,128)S(1)} all-to-all(f32[16,64,256]{2,1,0:T(8,128)S(1)} %broadcast_in_dim.69), channel_id=1, replica_groups=mesh['prow'=16,'pcol'=8] {'prow'}, dimensions={0} | all-to-all | bytes 2097152 | tf_op jit(solution)/shard_map/all_to_all | solution.py:54
  389.1 3.5 collective-permute-start.12
  394.9 3.5 all-to-all-start.22
  399.7 13.6 %all-to-all-done.22 = f32[4,512,128]{2,1,0:T(8,128)S(1)} async-done(((f32[4,512,128]{2,1,0:T(8,128)}), f32[4,512,128]{2,1,0:T(8,128)S(1)}, u32[]{:S(2)}, u32[]{:S(2)}) %all-to-all-start.22) | async-done | bytes 1048608 | tf_op jit(solution)/shard_map/all_to_all | solution.py:28
  (185 shorter events, 59.7 us)
Async XLA Ops:
  7.2 185.3 %all-gather.2.cloned.1.call-start = ((), (), s32[]{:S(2)}) async-start(), calls=%async_computation.23 | async-start | bytes 6684672 | tf_op jit(solution)/shard_map/all_gather | solution.py:64
  11.7 33.1 %copy-start.19 = (s32[98]{0:T(128)S(1)}, s32[98]{0:T(128)}, u32[]{:S(2)}) copy-start(s32[98]{0:T(128)} %param.7) | copy-start | bytes 1180
  39.9 16.6 %all-to-all-start.1 = ((f32[16,64,256]{2,1,0:T(8,128)}), f32[16,64,256]{2,1,0:T(8,128)S(1)}, u32[]{:S(2)}, u32[]{:S(2)}) async-start(f32[16,64,256]{2,1,0:T(8,128)} %broadcast_in_dim.48), calls=%async_computation.1 | async-start | bytes 2097152 | tf_op jit(solution)/shard_map/all_to_all | solution.py:54
  44.9 13.4 %copy-start.5 = (f32[16]{0:T(128)}, f32[16]{0:T(128)S(1)}, u32[]{:S(2)}) copy-start(f32[16]{0:T(128)S(1)} %slice.174) | copy-start | bytes 196
  58.4 13.5 %collective-permute-start = (f32[256,128]{1,0:T(8,128)S(1)}, f32[256,128]{1,0:T(8,128)S(1)}, u32[]{:S(2)}, u32[]{:S(2)}) collective-permute-start(f32[256,128]{1,0:T(8,128)S(1)} %dynamic-slice_bitcast_fusion.2), channel_id=1, source_target_pairs={{0,1},{1,0},{2,3},{3,2},{4,5},{5,4},{6,7},{7,6},{8,9},{9,8},{10,11... | collective-permute-start | bytes 393224 | tf_op jit(solution)/shard_map/ppermute | solution.py:42
  85.1 2.8 collective-permute-start.1
  106.8 13.0 %all-to-all-start.4 = ((f32[16,32,256]{2,1,0:T(8,128)}), f32[16,32,256]{2,1,0:T(8,128)S(1)}, u32[]{:S(2)}, u32[]{:S(2)}) async-start(f32[16,32,256]{2,1,0:T(8,128)} %broadcast_in_dim.50), calls=%async_computation.4 | async-start | bytes 1048576 | tf_op jit(solution)/shard_map/all_to_all | solution.py:54
  110.7 9.2 %copy-start.7 = (f32[16]{0:T(128)}, f32[16]{0:T(128)S(1)}, u32[]{:S(2)}) copy-start(f32[16]{0:T(128)S(1)} %slice.180) | copy-start | bytes 196
  119.8 26.2 %copy-start.1 = (f32[16,32,256]{2,1,0:T(8,128)}, f32[16,32,256]{2,1,0:T(8,128)S(1)}, u32[]{:S(2)}) copy-start(f32[16,32,256]{2,1,0:T(8,128)S(1)} %all-to-all-done.4) | copy-start | bytes 1572868
  121.4 4.2 collective-permute-start.2
  126.3 9.5 %all-to-all-start.5 = ((f32[4,128,128]{2,1,0:T(8,128)}), f32[4,128,128]{2,1,0:T(8,128)S(1)}, u32[]{:S(2)}, u32[]{:S(2)}) async-start(f32[4,128,128]{2,1,0:T(8,128)} %broadcast_in_dim.51), calls=%async_computation.5 | async-start | bytes 524288 | tf_op jit(solution)/shard_map/all_to_all | solution.py:28
  135.9 2.9 collective-permute-start.3
  138.3 29.7 %copy-start.17 = (f32[4]{0:T(128)}, f32[4]{0:T(128)S(1)}, u32[]{:S(2)}) copy-start(f32[4]{0:T(128)S(1)} %slice.194) | copy-start | bytes 52
  138.4 5.9 %copy-start.11 = (f32[16]{0:T(128)}, f32[16]{0:T(128)S(1)}, u32[]{:S(2)}) copy-start(f32[16]{0:T(128)S(1)} %slice.190) | copy-start | bytes 196
  138.5 18.3 %copy-start.13 = (f32[8]{0:T(128)}, f32[8]{0:T(128)S(1)}, u32[]{:S(2)}) copy-start(f32[8]{0:T(128)S(1)} %slice.192) | copy-start | bytes 100
  138.6 25.7 %copy-start.15 = (f32[4]{0:T(128)}, f32[4]{0:T(128)S(1)}, u32[]{:S(2)}) copy-start(f32[4]{0:T(128)S(1)} %slice.185) | copy-start | bytes 52
  138.7 14.3 %copy-start.9 = (f32[16]{0:T(128)}, f32[16]{0:T(128)S(1)}, u32[]{:S(2)}) copy-start(f32[16]{0:T(128)S(1)} %slice.171) | copy-start | bytes 196
  140.8 11.4 %all-to-all-start.6 = ((f32[16,16,256]{2,1,0:T(8,128)}), f32[16,16,256]{2,1,0:T(8,128)S(1)}, u32[]{:S(2)}, u32[]{:S(2)}) async-start(f32[16,16,256]{2,1,0:T(8,128)} %bitcast.19), calls=%async_computation.6 | async-start | bytes 524288 | tf_op jit(solution)/shard_map/all_to_all | solution.py:52
  153.0 11.3 %all-to-all-start.7 = ((f32[16,16,256]{2,1,0:T(8,128)}), f32[16,16,256]{2,1,0:T(8,128)S(1)}, u32[]{:S(2)}, u32[]{:S(2)}) async-start(f32[16,16,256]{2,1,0:T(8,128)} %broadcast_in_dim.52), calls=%async_computation.7 | async-start | bytes 524288 | tf_op jit(solution)/shard_map/all_to_all | solution.py:54
  165.6 3.6 collective-permute-start.4
  169.9 10.2 %all-to-all-start.8 = ((f32[4,128,128]{2,1,0:T(8,128)}), f32[4,128,128]{2,1,0:T(8,128)S(1)}, u32[]{:S(2)}, u32[]{:S(2)}) async-start(f32[4,128,128]{2,1,0:T(8,128)} %broadcast_in_dim.53), calls=%async_computation.8 | async-start | bytes 524288 | tf_op jit(solution)/shard_map/all_to_all | solution.py:28
  182.0 10.4 %all-to-all-start.9 = ((f32[16,4,640]{2,1,0:T(4,128)}), f32[16,4,640]{2,1,0:T(4,128)S(1)}, u32[]{:S(2)}, u32[]{:S(2)}) async-start(f32[16,4,640]{2,1,0:T(4,128)} %pad_maximum_fusion.1), calls=%async_computation.9 | async-start | bytes 327680 | tf_op jit(solution)/shard_map/all_to_all | solution.py:94
  192.4 0.7 copy-start.4
  196.7 1.7 copy-start
  198.4 2.9 collective-permute-start.5
  213.0 2.3 collective-permute-start.6
  216.1 8.8 %all-to-all-start.11 = ((f32[4,64,128]{2,1,0:T(8,128)}), f32[4,64,128]{2,1,0:T(8,128)}, u32[]{:S(2)}, u32[]{:S(2)}) async-start(f32[4,64,128]{2,1,0:T(8,128)} %broadcast_in_dim.55), calls=%async_computation.11 | async-start | bytes 262144 | tf_op jit(solution)/shard_map/all_to_all | solution.py:28
  225.8 21.5 %copy-start.18 = (f32[4]{0:T(128)S(1)}, f32[4]{0:T(128)}, u32[]{:S(2)}) copy-start(f32[4]{0:T(128)} %copy-done.17) | copy-start | bytes 52
  226.2 27.0 %copy-start.16 = (f32[4]{0:T(128)S(1)}, f32[4]{0:T(128)}, u32[]{:S(2)}) copy-start(f32[4]{0:T(128)} %copy-done.15) | copy-start | bytes 52
  239.0 3.9 collective-permute-start.7
  243.6 9.6 %all-to-all-start.13 = ((f32[4,128,128]{2,1,0:T(8,128)}), f32[4,128,128]{2,1,0:T(8,128)S(1)}, u32[]{:S(2)}, u32[]{:S(2)}) async-start(f32[4,128,128]{2,1,0:T(8,128)} %broadcast_in_dim.58), calls=%async_computation.13 | async-start | bytes 524288 | tf_op jit(solution)/shard_map/all_to_all | solution.py:28
  247.3 41.8 %copy-start.14 = (f32[8]{0:T(128)S(1)}, f32[8]{0:T(128)}, u32[]{:S(2)}) copy-start(f32[8]{0:T(128)} %copy-done.13) | copy-start | bytes 100
  255.1 11.0 %all-to-all-start.14 = ((f32[16,16,256]{2,1,0:T(8,128)}), f32[16,16,256]{2,1,0:T(8,128)S(1)}, u32[]{:S(2)}, u32[]{:S(2)}) async-start(f32[16,16,256]{2,1,0:T(8,128)} %bitcast.65), calls=%async_computation.14 | async-start | bytes 524288 | tf_op jit(solution)/shard_map/all_to_all | solution.py:52
  266.8 11.0 %all-to-all-start.15 = ((f32[16,16,256]{2,1,0:T(8,128)}), f32[16,16,256]{2,1,0:T(8,128)S(1)}, u32[]{:S(2)}, u32[]{:S(2)}) async-start(f32[16,16,256]{2,1,0:T(8,128)} %broadcast_in_dim.60), calls=%async_computation.15 | async-start | bytes 524288 | tf_op jit(solution)/shard_map/all_to_all | solution.py:54
  279.7 5.3 %collective-permute-start.8 = (f32[128,128]{1,0:T(8,128)S(1)}, f32[128,128]{1,0:T(8,128)S(1)}, u32[]{:S(2)}, u32[]{:S(2)}) collective-permute-start(f32[128,128]{1,0:T(8,128)S(1)} %dynamic-slice_bitcast_fusion.3), channel_id=1, source_target_pairs={{0,1},{1,0},{2,3},{3,2},{4,5},{5,4},{6,7},{7,6},{8,9},{9,8},{10,11... | collective-permute-start | bytes 196616 | tf_op jit(solution)/shard_map/ppermute | solution.py:42
  285.7 9.5 %all-to-all-start.16 = ((f32[4,128,128]{2,1,0:T(8,128)}), f32[4,128,128]{2,1,0:T(8,128)S(1)}, u32[]{:S(2)}, u32[]{:S(2)}) async-start(f32[4,128,128]{2,1,0:T(8,128)} %broadcast_in_dim.61), calls=%async_computation.16 | async-start | bytes 524288 | tf_op jit(solution)/shard_map/all_to_all | solution.py:28
  295.2 2.9 collective-permute-start.9
  298.1 28.0 %copy-start.2 = (f32[16,32,256]{2,1,0:T(8,128)S(1)}, f32[16,32,256]{2,1,0:T(8,128)}, u32[]{:S(2)}) copy-start(f32[16,32,256]{2,1,0:T(8,128)} %copy-done.1) | copy-start | bytes 1572868
  312.9 24.2 %copy-start.12 = (f32[16]{0:T(128)S(1)}, f32[16]{0:T(128)}, u32[]{:S(2)}) copy-start(f32[16]{0:T(128)} %copy-done.11) | copy-start | bytes 196
  327.0 11.7 %copy-start.10 = (f32[16]{0:T(128)S(1)}, f32[16]{0:T(128)}, u32[]{:S(2)}) copy-start(f32[16]{0:T(128)} %copy-done.9) | copy-start | bytes 196
  328.3 4.5 %collective-permute-start.10 = (f32[256,128]{1,0:T(8,128)S(1)}, f32[256,128]{1,0:T(8,128)S(1)}, u32[]{:S(2)}, u32[]{:S(2)}) collective-permute-start(f32[256,128]{1,0:T(8,128)S(1)} %dynamic-slice_bitcast_fusion.1), channel_id=1, source_target_pairs={{0,1},{1,0},{2,3},{3,2},{4,5},{5,4},{6,7},{7,6},{8,9},{9,8},{10,11... | collective-permute-start | bytes 393224 | tf_op jit(solution)/shard_map/ppermute | solution.py:42
  333.6 12.7 %all-to-all-start.19 = ((f32[4,256,128]{2,1,0:T(8,128)}), f32[4,256,128]{2,1,0:T(8,128)S(1)}, u32[]{:S(2)}, u32[]{:S(2)}) async-start(f32[4,256,128]{2,1,0:T(8,128)} %broadcast_in_dim.65), calls=%async_computation.19 | async-start | bytes 1048576 | tf_op jit(solution)/shard_map/all_to_all | solution.py:28
  337.1 10.6 %copy-start.8 = (f32[16]{0:T(128)S(1)}, f32[16]{0:T(128)}, u32[]{:S(2)}) copy-start(f32[16]{0:T(128)} %copy-done.7) | copy-start | bytes 196
  340.3 9.1 %copy-start.6 = (f32[16]{0:T(128)S(1)}, f32[16]{0:T(128)}, u32[]{:S(2)}) copy-start(f32[16]{0:T(128)} %copy-done.5) | copy-start | bytes 196
  346.3 2.9 collective-permute-start.11
  369.7 19.0 %copy-start.3 = (bf16[31,256,128]{2,1,0:T(8,128)(2,1)S(1)}, bf16[31,256,128]{2,1,0:T(8,128)(2,1)}, u32[]{:S(2)}) copy-start(bf16[31,256,128]{2,1,0:T(8,128)(2,1)} %param.6) | copy-start | bytes 6094852
  389.1 4.7 %collective-permute-start.12 = (f32[512,128]{1,0:T(8,128)S(1)}, f32[512,128]{1,0:T(8,128)S(1)}, u32[]{:S(2)}, u32[]{:S(2)}) collective-permute-start(f32[512,128]{1,0:T(8,128)S(1)} %dynamic-slice_bitcast_fusion), channel_id=1, source_target_pairs={{0,1},{1,0},{2,3},{3,2},{4,5},{5,4},{6,7},{7,6},{8,9},{9,8},{10,11... | collective-permute-start | bytes 786440 | tf_op jit(solution)/shard_map/ppermute | solution.py:42
  394.9 18.3 %all-to-all-start.22 = ((f32[4,512,128]{2,1,0:T(8,128)}), f32[4,512,128]{2,1,0:T(8,128)S(1)}, u32[]{:S(2)}, u32[]{:S(2)}) async-start(f32[4,512,128]{2,1,0:T(8,128)} %broadcast_in_dim.70), calls=%async_computation.22 | async-start | bytes 2097152 | tf_op jit(solution)/shard_map/all_to_all | solution.py:28
  413.3 3.7 collective-permute-start.13
Sparse Core Ops, SparseCore 0:
  10.2 76.8 all-gather.1

commit v3 on v2

--- a/solution.py
+++ b/solution.py
@@ -6,6 +6,9 @@
 LEV = 5
 ROWS = 16
 RING = [[0, 2, 4, 6], [1, 3, 5, 7]]
+RIGHT = [(i, (i + 2) % 8) for i in range(8)]
+ACROSS = [(i, (i + 4) % 8) for i in range(8)]
+LEFT = [(i, (i + 6) % 8) for i in range(8)]
 TWIN = [(i, i ^ 1) for i in range(8)]
 
 
@@ -24,6 +27,11 @@
 
 
 def one_shot_ring(values):
+    if values.size <= 32768:
+        across = lax.ppermute(values, "pcol", ACROSS)
+        right = lax.ppermute(values, "pcol", RIGHT)
+        left = lax.ppermute(values, "pcol", LEFT)
+        return (values + across) + (left + right)
     copies = jnp.broadcast_to(values[None], (4,) + values.shape)
     parts = lax.all_to_all(copies, "pcol", 0, 0, axis_index_groups=RING)
     return parts.sum(axis=0)
@@ -55,16 +63,18 @@
     return whole.reshape(shape)
 
 
+def gather_top(factor, inverse, live, after):
+    halves = factor[0:2].reshape(2, 128, 2, 128).transpose(0, 2, 1, 3).reshape(2, 256, 128)
+    top = jnp.concatenate([inverse[0:1], halves]).astype(jnp.float32)
+    top, after = lax.optimization_barrier((top, after))
+    scale = jnp.concatenate([jnp.ones((1,), jnp.float32), live[0:2]])
+    top = (lax.all_gather(top, "prow") * scale[:, None, None]).astype(jnp.bfloat16)
+    return top, after
+
+
 def per_device(rhs, factor, inverse, pattern):
     live = pattern.astype(jnp.float32)
     bf16 = jnp.bfloat16
-    halves = factor[0:2].reshape(2, 128, 2, 128).transpose(0, 2, 1, 3).reshape(2, 256, 128)
-    top = jnp.concatenate([inverse[0:1], halves]).astype(jnp.float32)
-    scale = jnp.concatenate([jnp.ones((1,), jnp.float32), live[0:2]])
-    top = (lax.all_gather(top, "prow") * scale[:, None, None]).astype(bf16)
-    inverse_top = top[:, 0]
-    factor_top = top[:, 1:].reshape(ROWS, 2, 2, 128, 128)
-
     partial_value = [[] for _ in range(LEV)]
     forward_levels = [None] * LEV
 
@@ -83,11 +93,18 @@
         residual = rhs[first : first + count]
         if tree_depth < LEV - 1:
             residual = residual - sum_columns(sum(partial_value[tree_depth]))
+        if tree_depth == 1:
+            residual, top = lax.optimization_barrier((residual, top))
         pieces = product(residual.astype(bf16), inverse[first : first + count], "nrc,nwc->nrw")
         if tree_depth > 1:
-            forward_levels[tree_depth] = sum_rows(pieces)
+            forward = sum_rows(pieces)
+            if tree_depth == LEV - 1:
+                top, forward = gather_top(factor, inverse, live, forward)
+            forward_levels[tree_depth] = forward
             push_up(forward_levels[tree_depth].astype(bf16), tree_depth)
 
+    inverse_top = top[:, 0]
+    factor_top = top[:, 1:].reshape(ROWS, 2, 2, 128, 128)
     here = (lax.axis_index("pcol") == 0).astype(jnp.float32)
     root_part = sum(partial_value[0])[0] - rhs[0] * here
     sent = jnp.concatenate([pieces[0], pieces[1], root_part], axis=1).reshape(ROWS, 4, 640)

time: 428 us -> 401 us (0.937)
  blocking collectives: 139 us -> 113 us
  matrix products: 41.9 us -> 34.6 us
  waiting for transfers between devices: 98.3 us -> 103 us
  other arithmetic: 10.9 us -> 15.4 us
    all_to_all x7 -> x1, waiting for transfers between devices: 42.1 us -> 12.5 us  [one_shot_ring(): parts = lax.all_to_all(copies, 'pcol', 0, 0, axis_index_groups=RING)]
    ppermute x0 -> x24, waiting for transfers between devices: none -> 28.4 us  [the longest x8 16.7 us: one_shot_ring(): across = lax.ppermute(values, 'pcol', ACROSS)]
    ppermute x0 -> x24, starting transfers between devices: none -> 25.1 us  [the longest x8 19.2 us: one_shot_ring(): left = lax.ppermute(values, 'pcol', LEFT)]
    all_to_all x7 -> x1, starting transfers between devices: 24.9 us -> 3.79 us  [one_shot_ring(): parts = lax.all_to_all(copies, 'pcol', 0, 0, axis_index_groups=RING)]
    all_to_all x2 -> x0, blocking collectives: 20.4 us -> none  [one_shot_ring(): parts = lax.all_to_all(copies, 'pcol', 0, 0, axis_index_groups=RING)]
    ppermute x5, starting transfers between devices: 27.2 us -> 17.9 us  [sum_columns(): mine = mine + lax.ppermute(other, 'pcol', TWIN)]
    dot_general x32, matrix products: 41.9 us -> 34.6 us  [product(): return jnp.einsum(form, left, right, preferred_element_type=jnp.float32)]
    all_to_all x4, waiting for transfers between devices: 29.7 us -> 36.6 us  [sum_rows(): whole = lax.all_to_all(copies, 'prow', 0, 0)]
  transfers between devices with their start and end apart: 29 -> 47, of which waited for: 23 -> 34; matrix products, arithmetic and copies ran while one was open for 11% -> 10% of each run, Pallas kernels for 0% -> 0%
where the time goes in v3:
time: 401 us; the launch traced here: 399 us
  blocking collectives  113 us (28%)
  waiting for transfers between devices  103 us (26%)
  starting transfers between devices  95 us (24%)
  matrix products  34.6 us (9%)
  local copies, waits for them, and re-layouts  22.9 us (6%)
  other arithmetic  15.4 us (4%)
  between operations  14.9 us (4%)
    all_to_all x4, blocking collectives, sum_rows(): part = lax.all_to_all(chunks, 'prow', 0, 0).sum(axis=0)  70.2 us
    all_to_all x4, waiting for transfers between devices, sum_rows(): whole = lax.all_to_all(copies, 'prow', 0, 0)  36.6 us
    dot_general x32, matrix products, product(): return jnp.einsum(form, left, right, preferred_element_type=jnp.float32)  34.6 us
    all_to_all x2, blocking collectives, sum_rows(): whole = lax.all_to_all(copies, 'prow', 0, 0)  31.9 us
    ppermute x8, starting transfers between devices, one_shot_ring(): left = lax.ppermute(values, 'pcol', LEFT)  19.2 us
    ppermute x5, starting transfers between devices, sum_columns(): mine = mine + lax.ppermute(other, 'pcol', TWIN)  17.9 us
    ppermute x8, waiting for transfers between devices, one_shot_ring(): across = lax.ppermute(values, 'pcol', ACROSS)  16.7 us
    all_to_all x4, starting transfers between devices, sum_rows(): whole = lax.all_to_all(copies, 'prow', 0, 0)  15.3 us
  transfers between devices with their start and end apart: 47, of which 34 were waited for; matrix products, arithmetic and copies ran while one was open for 10% of the time, Pallas kernels for 0%

profile of v3, /device:TPU:1, one launch (start us, length us, event | category | flops | bytes accessed | tf_op | source)
XLA Modules:
  0.0 399.0 jit_solution(7741516996276490414)
XLA Ops:
  7.2 1.9 fusion.33
  9.1 24.2 %all_to_all.75 = f32[16,64,256]{2,1,0:T(8,128)S(1)} all-to-all(f32[16,64,256]{2,1,0:T(8,128)S(1)} %fusion.33), channel_id=1, replica_groups=mesh['prow'=16,'pcol'=8] {'prow'}, dimensions={0} | all-to-all | bytes 2097152 | tf_op jit(solution)/shard_map/all_to_all | solution.py:60
  34.4 3.7 all-to-all-start.1
  39.2 13.6 %all-to-all-done.1 = f32[16,64,256]{2,1,0:T(8,128)S(1)} async-done(((f32[16,64,256]{2,1,0:T(8,128)}), f32[16,64,256]{2,1,0:T(8,128)S(1)}, u32[]{:S(2)}, u32[]{:S(2)}) %all-to-all-start.1) | async-done | bytes 1048608 | tf_op jit(solution)/shard_map/all_to_all | solution.py:62
  53.8 1.7 bitcast_reduce_fusion.1
  56.2 3.3 collective-permute-start
  65.2 1.7 collective-permute-done.3
  66.9 3.9 collective-permute-done.1
  74.4 13.6 %all_to_all.76 = f32[16,32,256]{2,1,0:T(8,128)S(1)} all-to-all(f32[16,32,256]{2,1,0:T(8,128)S(1)} %bitcast.217), channel_id=1, replica_groups=mesh['prow'=16,'pcol'=8] {'prow'}, dimensions={0} | all-to-all | bytes 1048576 | tf_op jit(solution)/shard_map/all_to_all | solution.py:60
  88.9 3.7 all-to-all-start.3
  92.8 1.7 bitcast_reduce_fusion
  94.6 12.3 %all-to-all-done.3 = f32[16,32,256]{2,1,0:T(8,128)S(1)} async-done(((f32[16,32,256]{2,1,0:T(8,128)}), f32[16,32,256]{2,1,0:T(8,128)S(1)}, u32[]{:S(2)}, u32[]{:S(2)}) %all-to-all-start.3) | async-done | bytes 524320 | tf_op jit(solution)/shard_map/all_to_all | solution.py:62
  108.5 3.3 collective-permute-start.5
  113.6 1.8 collective-permute-start.7
  117.5 2.6 collective-permute-done.6
  120.1 2.1 collective-permute-start.9
  123.1 1.9 fusion.60
  125.1 5.3 %all-to-all-start.4 = ((f32[16,16,256]{2,1,0:T(8,128)}), f32[16,16,256]{2,1,0:T(8,128)S(1)}, u32[]{:S(2)}, u32[]{:S(2)}) async-start(f32[16,16,256]{2,1,0:T(8,128)} %bitcast.22), calls=%async_computation.4 | async-start | bytes 524288 | tf_op jit(solution)/shard_map/all_to_all | solution.py:60
  130.4 1.7 fusion.6
  132.1 1.7 bitcast_reduce_fusion.2
  133.8 4.1 %all-to-all-done.4 = f32[16,16,256]{2,1,0:T(8,128)S(1)} async-done(((f32[16,16,256]{2,1,0:T(8,128)}), f32[16,16,256]{2,1,0:T(8,128)S(1)}, u32[]{:S(2)}, u32[]{:S(2)}) %all-to-all-start.4) | async-done | bytes 262176 | tf_op jit(solution)/shard_map/all_to_all | solution.py:60
  138.7 3.7 all-to-all-start.5
  145.2 4.6 %all-to-all-done.5 = f32[16,16,256]{2,1,0:T(8,128)S(1)} async-done(((f32[16,16,256]{2,1,0:T(8,128)}), f32[16,16,256]{2,1,0:T(8,128)S(1)}, u32[]{:S(2)}, u32[]{:S(2)}) %all-to-all-start.5) | async-done | bytes 262176 | tf_op jit(solution)/shard_map/all_to_all | solution.py:62
  151.1 3.0 collective-permute-start.10
  155.4 2.7 collective-permute-start.12
  158.1 2.1 collective-permute-done.13
  160.8 1.8 collective-permute-done.11
  163.6 5.5 %fusion = bf16[16,3,256,128]{3,2,0,1:T(8,128)(2,1)} fusion(f32[16,3,256,128]{3,2,1,0:T(8,128)} %bitcast.205, f32[3]{0:T(128)S(1)} %pad_maximum_fusion.3), kind=kLoop, calls=%fused_computation.1 | loop fusion | flops 3145728 | bytes 9437196 | tf_op jit(solution)/shard_map/convert_element_type | solution.py:71
  170.0 3.5 all-to-all-start.6
  173.5 1.7 slice.203
  175.3 5.1 %all-to-all-done.6 = f32[16,4,640]{2,1,0:T(4,128)S(1)} async-done(((f32[16,4,640]{2,1,0:T(4,128)}), f32[16,4,640]{2,1,0:T(4,128)S(1)}, u32[]{:S(2)}, u32[]{:S(2)}) %all-to-all-start.6) | async-done | bytes 163872 | tf_op jit(solution)/shard_map/all_to_all | solution.py:111
  181.2 3.1 collective-permute-start.14
  185.1 2.7 collective-permute-start.16
  189.1 3.0 collective-permute-done.15
  195.1 2.1 collective-permute-start.18
  198.1 2.7 collective-permute-start.20
  202.2 1.6 copy.34
  203.8 1.6 copy.35
  206.4 11.3 %all_to_all.77 = f32[16,4,1408]{2,1,0:T(4,128)} all-to-all(f32[16,4,1408]{2,1,0:T(4,128)S(1)} %pad_maximum_fusion), channel_id=1, replica_groups=mesh['prow'=16,'pcol'=8] {'prow'}, dimensions={0} | all-to-all | bytes 720896 | tf_op jit(solution)/shard_map/all_to_all | solution.py:128
  219.0 3.1 collective-permute-start.22
  223.3 2.5 collective-permute-start.24
  228.3 2.1 collective-permute-done.23
  230.4 1.8 fusion.7
  232.3 4.2 %all-to-all-start.8 = ((f32[16,16,256]{2,1,0:T(8,128)}), f32[16,16,256]{2,1,0:T(8,128)}, u32[]{:S(2)}, u32[]{:S(2)}) async-start(f32[16,16,256]{2,1,0:T(8,128)} %bitcast.223), calls=%async_computation.8 | async-start | bytes 524288 | tf_op jit(solution)/shard_map/all_to_all | solution.py:60
  237.1 6.7 %all-to-all-done.8 = f32[16,16,256]{2,1,0:T(8,128)} async-done(((f32[16,16,256]{2,1,0:T(8,128)}), f32[16,16,256]{2,1,0:T(8,128)}, u32[]{:S(2)}, u32[]{:S(2)}) %all-to-all-start.8) | async-done | bytes 262176 | tf_op jit(solution)/shard_map/all_to_all | solution.py:60
  245.6 4.2 %all-to-all-start.9 = ((f32[16,16,256]{2,1,0:T(8,128)}), f32[16,16,256]{2,1,0:T(8,128)}, u32[]{:S(2)}, u32[]{:S(2)}) async-start(f32[16,16,256]{2,1,0:T(8,128)} %broadcast_in_dim.38), calls=%async_computation.9 | async-start | bytes 524288 | tf_op jit(solution)/shard_map/all_to_all | solution.py:62
  251.0 6.1 %all-to-all-done.9 = f32[16,16,256]{2,1,0:T(8,128)} async-done(((f32[16,16,256]{2,1,0:T(8,128)}), f32[16,16,256]{2,1,0:T(8,128)}, u32[]{:S(2)}, u32[]{:S(2)}) %all-to-all-start.9) | async-done | bytes 262176 | tf_op jit(solution)/shard_map/all_to_all | solution.py:62
  257.1 1.8 bitcast_dynamic-update-slice_fusion.1
  259.1 4.4 %collective-permute-start.26 = (f32[128,128]{1,0:T(8,128)S(1)}, f32[128,128]{1,0:T(8,128)S(1)}, u32[]{:S(2)}, u32[]{:S(2)}) collective-permute-start(f32[128,128]{1,0:T(8,128)S(1)} %dynamic-slice_bitcast_fusion.3), channel_id=1, source_target_pairs={{0,1},{1,0},{2,3},{3,2},{4,5},{5,4},{6,7},{7,6},{8,9},{9,8},{10,11... | collective-permute-start | bytes 196616 | tf_op jit(solution)/shard_map/ppermute | solution.py:50
  264.5 2.7 collective-permute-start.28
  269.2 2.6 collective-permute-done.27
  271.8 2.1 collective-permute-start.30
  277.2 13.4 %all_to_all.78 = f32[16,32,256]{2,1,0:T(8,128)} all-to-all(f32[16,32,256]{2,1,0:T(8,128)S(1)} %bitcast.219), channel_id=1, replica_groups=mesh['prow'=16,'pcol'=8] {'prow'}, dimensions={0} | all-to-all | bytes 1048576 | tf_op jit(solution)/shard_map/all_to_all | solution.py:60
  291.8 13.4 %all_to_all.79 = f32[16,32,256]{2,1,0:T(8,128)S(1)} all-to-all(f32[16,32,256]{2,1,0:T(8,128)S(1)} %broadcast_in_dim.41), channel_id=1, replica_groups=mesh['prow'=16,'pcol'=8] {'prow'}, dimensions={0} | all-to-all | bytes 1048576 | tf_op jit(solution)/shard_map/all_to_all | solution.py:62
  305.2 1.9 bitcast_dynamic-update-slice_fusion
  308.4 3.5 collective-permute-start.31
  313.6 2.7 collective-permute-start.33
  316.6 3.2 collective-permute-done.34
  319.9 1.6 collective-permute-done.33
  325.2 18.9 %all_to_all.80 = f32[16,64,256]{2,1,0:T(8,128)S(1)} all-to-all(f32[16,64,256]{2,1,0:T(8,128)S(1)} %fusion.1), channel_id=1, replica_groups=mesh['prow'=16,'pcol'=8] {'prow'}, dimensions={0} | all-to-all | bytes 2097152 | tf_op jit(solution)/shard_map/all_to_all | solution.py:60
  344.3 18.5 %all_to_all.81 = f32[16,64,256]{2,1,0:T(8,128)S(1)} all-to-all(f32[16,64,256]{2,1,0:T(8,128)S(1)} %broadcast_in_dim.45), channel_id=1, replica_groups=mesh['prow'=16,'pcol'=8] {'prow'}, dimensions={0} | all-to-all | bytes 2097152 | tf_op jit(solution)/shard_map/all_to_all | solution.py:62
  363.2 3.3 collective-permute-start.36
  368.8 3.8 all-to-all-start.14
  374.6 12.5 %all-to-all-done.14 = f32[4,512,128]{2,1,0:T(8,128)S(1)} async-done(((f32[4,512,128]{2,1,0:T(8,128)}), f32[4,512,128]{2,1,0:T(8,128)S(1)}, u32[]{:S(2)}, u32[]{:S(2)}) %all-to-all-start.14) | async-done | bytes 1048608 | tf_op jit(solution)/shard_map/all_to_all | solution.py:36
  (208 shorter events, 71.2 us)
Async XLA Ops:
  9.0 29.1 %slice-start.2 = ((bf16[98,128,256]{2,1,0:T(8,128)(2,1)}), bf16[2,128,256]{2,1,0:T(8,128)(2,1)S(1)}, s32[]{:S(2)}) async-start(bf16[98,128,256]{2,1,0:T(8,128)(2,1)} %param.5), calls=%async_computation.18 | async-start | bytes 262144 | tf_op jit(solution)/shard_map/slice | solution.py:67
  33.3 5.1 %slice-start.3 = ((bf16[31,256,128]{2,1,0:T(8,128)(2,1)}), bf16[1,256,128]{2,1,0:T(8,128)(2,1)S(1)}, s32[]{:S(2)}) async-start(bf16[31,256,128]{2,1,0:T(8,128)(2,1)} %param.6), calls=%async_computation.19 | async-start | bytes 131072 | tf_op jit(solution)/shard_map/slice | solution.py:68
  33.3 19.6 %copy-start.13 = (s32[98]{0:T(128)S(1)}, s32[98]{0:T(128)}, u32[]{:S(2)}) copy-start(s32[98]{0:T(128)} %param.7) | copy-start | bytes 1180
  34.4 18.4 %all-to-all-start.1 = ((f32[16,64,256]{2,1,0:T(8,128)}), f32[16,64,256]{2,1,0:T(8,128)S(1)}, u32[]{:S(2)}, u32[]{:S(2)}) async-start(f32[16,64,256]{2,1,0:T(8,128)} %broadcast_in_dim.32), calls=%async_computation.1 | async-start | bytes 2097152 | tf_op jit(solution)/shard_map/all_to_all | solution.py:62
  38.1 125.5 %all-gather.3.cloned.1.call-start = ((), (), s32[]{:S(2)}) async-start(), calls=%async_computation.15 | async-start | bytes 6684672 | tf_op jit(solution)/shard_map/all_gather | solution.py:71
  38.4 34.7 %copy-start.1 = (bf16[31,256,128]{2,1,0:T(8,128)(2,1)S(1)}, bf16[31,256,128]{2,1,0:T(8,128)(2,1)}, u32[]{:S(2)}) copy-start(bf16[31,256,128]{2,1,0:T(8,128)(2,1)} %param.6) | copy-start | bytes 6094852
  53.0 0.8 copy-start.11
  56.2 4.5 %collective-permute-start = (f32[256,128]{1,0:T(8,128)}, f32[256,128]{1,0:T(8,128)S(1)}, u32[]{:S(2)}, u32[]{:S(2)}) collective-permute-start(f32[256,128]{1,0:T(8,128)} %dynamic-slice_bitcast_fusion.2), channel_id=1, source_target_pairs={{0,1},{1,0},{2,3},{3,2},{4,5},{5,4},{6,7},{7,6},{8,9},{9,8},{10,11... | collective-permute-start | bytes 393224 | tf_op jit(solution)/shard_map/ppermute | solution.py:50
  60.8 6.1 %collective-permute-start.3 = (f32[256,128]{1,0:T(8,128)S(1)}, f32[256,128]{1,0:T(8,128)S(1)}, u32[]{:S(2)}, u32[]{:S(2)}) collective-permute-start(f32[256,128]{1,0:T(8,128)S(1)} %bitcast_add_fusion.2), channel_id=1, source_target_pairs={{0,2},{1,3},{2,4},{3,5},{4,6},{5,7},{6,0},{7,1},{8,10},{9,11},{10,... | collective-permute-start | bytes 393224 | tf_op jit(solution)/shard_map/ppermute | solution.py:32
  62.1 4.8 %collective-permute-start.2 = (f32[256,128]{1,0:T(8,128)S(1)}, f32[256,128]{1,0:T(8,128)S(1)}, u32[]{:S(2)}, u32[]{:S(2)}) collective-permute-start(f32[256,128]{1,0:T(8,128)S(1)} %bitcast_add_fusion.2), channel_id=1, source_target_pairs={{0,6},{1,7},{2,0},{3,1},{4,2},{5,3},{6,4},{7,5},{8,14},{9,15},{10,... | collective-permute-start | bytes 393224 | tf_op jit(solution)/shard_map/ppermute | solution.py:33
  63.7 7.2 %collective-permute-start.1 = (f32[256,128]{1,0:T(8,128)S(1)}, f32[256,128]{1,0:T(8,128)S(1)}, u32[]{:S(2)}, u32[]{:S(2)}) collective-permute-start(f32[256,128]{1,0:T(8,128)S(1)} %bitcast_add_fusion.2), channel_id=1, source_target_pairs={{0,4},{1,5},{2,6},{3,7},{4,0},{5,1},{6,2},{7,3},{8,12},{9,13},{10,... | collective-permute-start | bytes 393224 | tf_op jit(solution)/shard_map/ppermute | solution.py:31
  70.9 2.3 collective-permute-start.4
  74.4 18.4 %copy-start.12 = (bf16[16,64,256]{2,1,0:T(8,128)(2,1)S(1)}, bf16[16,64,256]{2,1,0:T(8,128)(2,1)}, u32[]{:S(2)}) copy-start(bf16[16,64,256]{2,1,0:T(8,128)(2,1)} %copy-done.11) | copy-start | bytes 1572868
  88.9 18.0 %all-to-all-start.3 = ((f32[16,32,256]{2,1,0:T(8,128)}), f32[16,32,256]{2,1,0:T(8,128)S(1)}, u32[]{:S(2)}, u32[]{:S(2)}) async-start(f32[16,32,256]{2,1,0:T(8,128)} %broadcast_in_dim.33), calls=%async_computation.3 | async-start | bytes 1048576 | tf_op jit(solution)/shard_map/all_to_all | solution.py:62
  106.9 25.2 %copy-start = (f32[16,32,256]{2,1,0:T(8,128)}, f32[16,32,256]{2,1,0:T(8,128)S(1)}, u32[]{:S(2)}) copy-start(f32[16,32,256]{2,1,0:T(8,128)S(1)} %all-to-all-done.3) | copy-start | bytes 1572868
  108.5 4.2 %collective-permute-start.5 = (f32[128,128]{1,0:T(8,128)S(1)}, f32[128,128]{1,0:T(8,128)S(1)}, u32[]{:S(2)}, u32[]{:S(2)}) collective-permute-start(f32[128,128]{1,0:T(8,128)S(1)} %dynamic-slice_bitcast_fusion.4), channel_id=1, source_target_pairs={{0,1},{1,0},{2,3},{3,2},{4,5},{5,4},{6,7},{7,6},{8,9},{9,8},{10,11... | collective-permute-start | bytes 196616 | tf_op jit(solution)/shard_map/ppermute | solution.py:50
  112.7 4.8 %collective-permute-start.8 = (f32[128,128]{1,0:T(8,128)S(1)}, f32[128,128]{1,0:T(8,128)S(1)}, u32[]{:S(2)}, u32[]{:S(2)}) collective-permute-start(f32[128,128]{1,0:T(8,128)S(1)} %bitcast_add_fusion.4), channel_id=1, source_target_pairs={{0,2},{1,3},{2,4},{3,5},{4,6},{5,7},{6,0},{7,1},{8,10},{9,11},{10,... | collective-permute-start | bytes 196616 | tf_op jit(solution)/shard_map/ppermute | solution.py:32
  113.6 3.9 collective-permute-start.7
  115.4 4.7 %collective-permute-start.6 = (f32[128,128]{1,0:T(8,128)S(1)}, f32[128,128]{1,0:T(8,128)S(1)}, u32[]{:S(2)}, u32[]{:S(2)}) collective-permute-start(f32[128,128]{1,0:T(8,128)S(1)} %bitcast_add_fusion.4), channel_id=1, source_target_pairs={{0,4},{1,5},{2,6},{3,7},{4,0},{5,1},{6,2},{7,3},{8,12},{9,13},{10,... | collective-permute-start | bytes 196616 | tf_op jit(solution)/shard_map/ppermute | solution.py:31
  120.1 3.0 collective-permute-start.9
  125.1 12.9 %all-to-all-start.4 = ((f32[16,16,256]{2,1,0:T(8,128)}), f32[16,16,256]{2,1,0:T(8,128)S(1)}, u32[]{:S(2)}, u32[]{:S(2)}) async-start(f32[16,16,256]{2,1,0:T(8,128)} %bitcast.22), calls=%async_computation.4 | async-start | bytes 524288 | tf_op jit(solution)/shard_map/all_to_all | solution.py:60
  138.7 11.1 %all-to-all-start.5 = ((f32[16,16,256]{2,1,0:T(8,128)}), f32[16,16,256]{2,1,0:T(8,128)S(1)}, u32[]{:S(2)}, u32[]{:S(2)}) async-start(f32[16,16,256]{2,1,0:T(8,128)} %broadcast_in_dim.34), calls=%async_computation.5 | async-start | bytes 524288 | tf_op jit(solution)/shard_map/all_to_all | solution.py:62
  149.8 19.3 %copy-start.6 = (f32[16,16,256]{2,1,0:T(8,128)}, f32[16,16,256]{2,1,0:T(8,128)S(1)}, u32[]{:S(2)}) copy-start(f32[16,16,256]{2,1,0:T(8,128)S(1)} %all-to-all-done.5) | copy-start | bytes 786436
  151.1 4.2 %collective-permute-start.10 = (f32[128,128]{1,0:T(8,128)S(1)}, f32[128,128]{1,0:T(8,128)S(1)}, u32[]{:S(2)}, u32[]{:S(2)}) collective-permute-start(f32[128,128]{1,0:T(8,128)S(1)} %bitcast.252), channel_id=1, source_target_pairs={{0,1},{1,0},{2,3},{3,2},{4,5},{5,4},{6,7},{7,6},{8,9},{9,8},{10,11... | collective-permute-start | bytes 196616 | tf_op jit(solution)/shard_map/ppermute | solution.py:44
  155.3 4.9 %collective-permute-start.13 = (f32[128,128]{1,0:T(8,128)S(1)}, f32[128,128]{1,0:T(8,128)S(1)}, u32[]{:S(2)}, u32[]{:S(2)}) collective-permute-start(f32[128,128]{1,0:T(8,128)S(1)} %bitcast_add_fusion.6), channel_id=1, source_target_pairs={{0,2},{1,3},{2,4},{3,5},{4,6},{5,7},{6,0},{7,1},{8,10},{9,11},{10,... | collective-permute-start | bytes 196616 | tf_op jit(solution)/shard_map/ppermute | solution.py:32
  155.4 5.5 %collective-permute-start.12 = (f32[128,128]{1,0:T(8,128)S(1)}, f32[128,128]{1,0:T(8,128)S(1)}, u32[]{:S(2)}, u32[]{:S(2)}) collective-permute-start(f32[128,128]{1,0:T(8,128)S(1)} %bitcast_add_fusion.6), channel_id=1, source_target_pairs={{0,6},{1,7},{2,0},{3,1},{4,2},{5,3},{6,4},{7,5},{8,14},{9,15},{10,... | collective-permute-start | bytes 196616 | tf_op jit(solution)/shard_map/ppermute | solution.py:33
  158.0 4.6 %collective-permute-start.11 = (f32[128,128]{1,0:T(8,128)S(1)}, f32[128,128]{1,0:T(8,128)S(1)}, u32[]{:S(2)}, u32[]{:S(2)}) collective-permute-start(f32[128,128]{1,0:T(8,128)S(1)} %bitcast_add_fusion.6), channel_id=1, source_target_pairs={{0,4},{1,5},{2,6},{3,7},{4,0},{5,1},{6,2},{7,3},{8,12},{9,13},{10,... | collective-permute-start | bytes 196616 | tf_op jit(solution)/shard_map/ppermute | solution.py:31
  163.6 5.5 %copy-start.2 = (bf16[31,256,128]{2,1,0:T(8,128)(2,1)S(1)}, bf16[31,256,128]{2,1,0:T(8,128)(2,1)}, u32[]{:S(2)}) copy-start(bf16[31,256,128]{2,1,0:T(8,128)(2,1)} %param.6) | copy-start | bytes 6094852
  170.0 10.4 %all-to-all-start.6 = ((f32[16,4,640]{2,1,0:T(4,128)}), f32[16,4,640]{2,1,0:T(4,128)S(1)}, u32[]{:S(2)}, u32[]{:S(2)}) async-start(f32[16,4,640]{2,1,0:T(4,128)} %pad_maximum_fusion.1), calls=%async_computation.6 | async-start | bytes 327680 | tf_op jit(solution)/shard_map/all_to_all | solution.py:111
  181.2 3.9 collective-permute-start.14
  185.1 4.0 collective-permute-start.17
  185.1 4.0 collective-permute-start.16
  187.8 4.3 %collective-permute-start.15 = (f32[64,128]{1,0:T(8,128)S(1)}, f32[64,128]{1,0:T(8,128)S(1)}, u32[]{:S(2)}, u32[]{:S(2)}) collective-permute-start(f32[64,128]{1,0:T(8,128)S(1)} %add.211), channel_id=1, source_target_pairs={{0,4},{1,5},{2,6},{3,7},{4,0},{5,1},{6,2},{7,3},{8,12},{9,13},{10,... | collective-permute-start | bytes 98312 | tf_op jit(solution)/shard_map/ppermute | solution.py:31
  195.1 2.9 collective-permute-start.18
  198.1 7.4 %collective-permute-start.21 = (f32[64,128]{1,0:T(8,128)S(1)}, f32[64,128]{1,0:T(8,128)S(1)}, u32[]{:S(2)}, u32[]{:S(2)}) collective-permute-start(f32[64,128]{1,0:T(8,128)S(1)} %add.215), channel_id=1, source_target_pairs={{0,2},{1,3},{2,4},{3,5},{4,6},{5,7},{6,0},{7,1},{8,10},{9,11},{10,... | collective-permute-start | bytes 98312 | tf_op jit(solution)/shard_map/ppermute | solution.py:32
  198.1 7.4 %collective-permute-start.20 = (f32[64,128]{1,0:T(8,128)S(1)}, f32[64,128]{1,0:T(8,128)S(1)}, u32[]{:S(2)}, u32[]{:S(2)}) collective-permute-start(f32[64,128]{1,0:T(8,128)S(1)} %add.215), channel_id=1, source_target_pairs={{0,6},{1,7},{2,0},{3,1},{4,2},{5,3},{6,4},{7,5},{8,14},{9,15},{10,... | collective-permute-start | bytes 98312 | tf_op jit(solution)/shard_map/ppermute | solution.py:33
  200.7 4.7 %collective-permute-start.19 = (f32[64,128]{1,0:T(8,128)S(1)}, f32[64,128]{1,0:T(8,128)S(1)}, u32[]{:S(2)}, u32[]{:S(2)}) collective-permute-start(f32[64,128]{1,0:T(8,128)S(1)} %add.215), channel_id=1, source_target_pairs={{0,4},{1,5},{2,6},{3,7},{4,0},{5,1},{6,2},{7,3},{8,12},{9,13},{10,... | collective-permute-start | bytes 98312 | tf_op jit(solution)/shard_map/ppermute | solution.py:31
  206.3 12.6 %copy-start.3 = (bf16[31,256,128]{2,1,0:T(8,128)(2,1)S(1)}, bf16[31,256,128]{2,1,0:T(8,128)(2,1)}, u32[]{:S(2)}) copy-start(bf16[31,256,128]{2,1,0:T(8,128)(2,1)} %param.6) | copy-start | bytes 6094852
  218.8 40.3 %copy-start.5 = (f32[64,1408]{1,0:T(8,128)}, f32[64,1408]{1,0:T(8,128)S(1)}, u32[]{:S(2)}) copy-start(f32[64,1408]{1,0:T(8,128)S(1)} %reshape.225) | copy-start | bytes 1081348
  219.0 4.0 collective-permute-start.22
  223.0 5.2 %collective-permute-start.25 = (f32[128,128]{1,0:T(8,128)S(1)}, f32[128,128]{1,0:T(8,128)S(1)}, u32[]{:S(2)}, u32[]{:S(2)}) collective-permute-start(f32[128,128]{1,0:T(8,128)S(1)} %bitcast_add_fusion.5), channel_id=1, source_target_pairs={{0,2},{1,3},{2,4},{3,5},{4,6},{5,7},{6,0},{7,1},{8,10},{9,11},{10,... | collective-permute-start | bytes 196616 | tf_op jit(solution)/shard_map/ppermute | solution.py:32
  223.3 5.0 %collective-permute-start.24 = (f32[128,128]{1,0:T(8,128)S(1)}, f32[128,128]{1,0:T(8,128)S(1)}, u32[]{:S(2)}, u32[]{:S(2)}) collective-permute-start(f32[128,128]{1,0:T(8,128)S(1)} %bitcast_add_fusion.5), channel_id=1, source_target_pairs={{0,6},{1,7},{2,0},{3,1},{4,2},{5,3},{6,4},{7,5},{8,14},{9,15},{10,... | collective-permute-start | bytes 196616 | tf_op jit(solution)/shard_map/ppermute | solution.py:33
  225.8 4.6 %collective-permute-start.23 = (f32[128,128]{1,0:T(8,128)S(1)}, f32[128,128]{1,0:T(8,128)S(1)}, u32[]{:S(2)}, u32[]{:S(2)}) collective-permute-start(f32[128,128]{1,0:T(8,128)S(1)} %bitcast_add_fusion.5), channel_id=1, source_target_pairs={{0,4},{1,5},{2,6},{3,7},{4,0},{5,1},{6,2},{7,3},{8,12},{9,13},{10,... | collective-permute-start | bytes 196616 | tf_op jit(solution)/shard_map/ppermute | solution.py:31
  230.4 1.9 copy-start.9
  232.3 11.6 %all-to-all-start.8 = ((f32[16,16,256]{2,1,0:T(8,128)}), f32[16,16,256]{2,1,0:T(8,128)}, u32[]{:S(2)}, u32[]{:S(2)}) async-start(f32[16,16,256]{2,1,0:T(8,128)} %bitcast.223), calls=%async_computation.8 | async-start | bytes 524288 | tf_op jit(solution)/shard_map/all_to_all | solution.py:60
  245.6 11.5 %all-to-all-start.9 = ((f32[16,16,256]{2,1,0:T(8,128)}), f32[16,16,256]{2,1,0:T(8,128)}, u32[]{:S(2)}, u32[]{:S(2)}) async-start(f32[16,16,256]{2,1,0:T(8,128)} %broadcast_in_dim.38), calls=%async_computation.9 | async-start | bytes 524288 | tf_op jit(solution)/shard_map/all_to_all | solution.py:62
  259.1 5.3 %collective-permute-start.26 = (f32[128,128]{1,0:T(8,128)S(1)}, f32[128,128]{1,0:T(8,128)S(1)}, u32[]{:S(2)}, u32[]{:S(2)}) collective-permute-start(f32[128,128]{1,0:T(8,128)S(1)} %dynamic-slice_bitcast_fusion.3), channel_id=1, source_target_pairs={{0,1},{1,0},{2,3},{3,2},{4,5},{5,4},{6,7},{7,6},{8,9},{9,8},{10,11... | collective-permute-start | bytes 196616 | tf_op jit(solution)/shard_map/ppermute | solution.py:50
  264.4 4.4 %collective-permute-start.29 = (f32[128,128]{1,0:T(8,128)S(1)}, f32[128,128]{1,0:T(8,128)S(1)}, u32[]{:S(2)}, u32[]{:S(2)}) collective-permute-start(f32[128,128]{1,0:T(8,128)S(1)} %bitcast_add_fusion.3), channel_id=1, source_target_pairs={{0,2},{1,3},{2,4},{3,5},{4,6},{5,7},{6,0},{7,1},{8,10},{9,11},{10,... | collective-permute-start | bytes 196616 | tf_op jit(solution)/shard_map/ppermute | solution.py:32
  264.5 4.7 %collective-permute-start.28 = (f32[128,128]{1,0:T(8,128)S(1)}, f32[128,128]{1,0:T(8,128)S(1)}, u32[]{:S(2)}, u32[]{:S(2)}) collective-permute-start(f32[128,128]{1,0:T(8,128)S(1)} %bitcast_add_fusion.3), channel_id=1, source_target_pairs={{0,6},{1,7},{2,0},{3,1},{4,2},{5,3},{6,4},{7,5},{8,14},{9,15},{10,... | collective-permute-start | bytes 196616 | tf_op jit(solution)/shard_map/ppermute | solution.py:33
  267.2 4.6 %collective-permute-start.27 = (f32[128,128]{1,0:T(8,128)S(1)}, f32[128,128]{1,0:T(8,128)S(1)}, u32[]{:S(2)}, u32[]{:S(2)}) collective-permute-start(f32[128,128]{1,0:T(8,128)S(1)} %bitcast_add_fusion.3), channel_id=1, source_target_pairs={{0,4},{1,5},{2,6},{3,7},{4,0},{5,1},{6,2},{7,3},{8,12},{9,13},{10,... | collective-permute-start | bytes 196616 | tf_op jit(solution)/shard_map/ppermute | solution.py:31
  267.3 49.0 %slice-start = ((s8[6422528]{0:T(1024)(128)(4,1)}), s8[2228224]{0:T(1024)(128)(4,1)S(1)}, s32[]{:S(2)}) async-start(s8[6422528]{0:T(1024)(128)(4,1)} %bitcast.203), calls=%async_computation.16 | async-start | bytes 4456448
  271.8 3.4 collective-permute-start.30
  291.7 24.6 %slice-start.1 = ((s8[6422528]{0:T(1024)(128)(4,1)}), s8[4194304]{0:T(1024)(128)(4,1)S(1)}, s32[]{:S(2)}) async-start(s8[6422528]{0:T(1024)(128)(4,1)} %bitcast.203), calls=%async_computation.17 | async-start | bytes 8388608
  308.4 5.1 %collective-permute-start.31 = (f32[256,128]{1,0:T(8,128)S(1)}, f32[256,128]{1,0:T(8,128)S(1)}, u32[]{:S(2)}, u32[]{:S(2)}) collective-permute-start(f32[256,128]{1,0:T(8,128)S(1)} %dynamic-slice_bitcast_fusion.1), channel_id=1, source_target_pairs={{0,1},{1,0},{2,3},{3,2},{4,5},{5,4},{6,7},{7,6},{8,9},{9,8},{10,11... | collective-permute-start | bytes 393224 | tf_op jit(solution)/shard_map/ppermute | solution.py:50
  313.5 6.4 %collective-permute-start.34 = (f32[256,128]{1,0:T(8,128)S(1)}, f32[256,128]{1,0:T(8,128)S(1)}, u32[]{:S(2)}, u32[]{:S(2)}) collective-permute-start(f32[256,128]{1,0:T(8,128)S(1)} %bitcast_add_fusion.1), channel_id=1, source_target_pairs={{0,2},{1,3},{2,4},{3,5},{4,6},{5,7},{6,0},{7,1},{8,10},{9,11},{10,... | collective-permute-start | bytes 393224 | tf_op jit(solution)/shard_map/ppermute | solution.py:32
  313.6 7.9 %collective-permute-start.33 = (f32[256,128]{1,0:T(8,128)S(1)}, f32[256,128]{1,0:T(8,128)S(1)}, u32[]{:S(2)}, u32[]{:S(2)}) collective-permute-start(f32[256,128]{1,0:T(8,128)S(1)} %bitcast_add_fusion.1), channel_id=1, source_target_pairs={{0,6},{1,7},{2,0},{3,1},{4,2},{5,3},{6,4},{7,5},{8,14},{9,15},{10,... | collective-permute-start | bytes 393224 | tf_op jit(solution)/shard_map/ppermute | solution.py:33
  316.3 6.0 %collective-permute-start.32 = (f32[256,128]{1,0:T(8,128)S(1)}, f32[256,128]{1,0:T(8,128)S(1)}, u32[]{:S(2)}, u32[]{:S(2)}) collective-permute-start(f32[256,128]{1,0:T(8,128)S(1)} %bitcast_add_fusion.1), channel_id=1, source_target_pairs={{0,4},{1,5},{2,6},{3,7},{4,0},{5,1},{6,2},{7,3},{8,12},{9,13},{10,... | collective-permute-start | bytes 393224 | tf_op jit(solution)/shard_map/ppermute | solution.py:31
  322.3 2.5 collective-permute-start.35
  344.2 18.6 %copy-start.4 = (bf16[31,256,128]{2,1,0:T(8,128)(2,1)S(1)}, bf16[31,256,128]{2,1,0:T(8,128)(2,1)}, u32[]{:S(2)}) copy-start(bf16[31,256,128]{2,1,0:T(8,128)(2,1)} %param.6) | copy-start | bytes 6094852
  363.1 10.8 %copy-start.10 = (f32[128,128]{1,0:T(8,128)S(1)}, f32[128,128]{1,0:T(8,128)}, u32[]{:S(2)}) copy-start(f32[128,128]{1,0:T(8,128)} %copy-done.9) | copy-start | bytes 196612
  363.2 25.6 %copy-start.8 = (f32[2,128,128]{2,1,0:T(8,128)S(1)}, f32[2,128,128]{2,1,0:T(8,128)}, u32[]{:S(2)}) copy-start(f32[2,128,128]{2,1,0:T(8,128)} %copy-done.7) | copy-start | bytes 393220
  363.2 4.5 %collective-permute-start.36 = (f32[512,128]{1,0:T(8,128)S(1)}, f32[512,128]{1,0:T(8,128)S(1)}, u32[]{:S(2)}, u32[]{:S(2)}) collective-permute-start(f32[512,128]{1,0:T(8,128)S(1)} %dynamic-slice_bitcast_fusion), channel_id=1, source_target_pairs={{0,1},{1,0},{2,3},{3,2},{4,5},{5,4},{6,7},{7,6},{8,9},{9,8},{10,11... | collective-permute-start | bytes 786440 | tf_op jit(solution)/shard_map/ppermute | solution.py:50
  368.8 18.3 %all-to-all-start.14 = ((f32[4,512,128]{2,1,0:T(8,128)}), f32[4,512,128]{2,1,0:T(8,128)S(1)}, u32[]{:S(2)}, u32[]{:S(2)}) async-start(f32[4,512,128]{2,1,0:T(8,128)} %broadcast_in_dim.46), calls=%async_computation.14 | async-start | bytes 2097152 | tf_op jit(solution)/shard_map/all_to_all | solution.py:36
  387.2 4.1 %collective-permute-start.37 = (f32[512,128]{1,0:T(8,128)S(1)}, f32[512,128]{1,0:T(8,128)S(1)}, u32[]{:S(2)}, u32[]{:S(2)}) collective-permute-start(f32[512,128]{1,0:T(8,128)S(1)} %reduce_sum.181), channel_id=1, source_target_pairs={{0,1},{1,0},{2,3},{3,2},{4,5},{5,4},{6,7},{7,6},{8,9},{9,8},{10,11... | collective-permute-start | bytes 786440 | tf_op jit(solution)/shard_map/ppermute | solution.py:52
  (1 other events, 0.7 us)
Sparse Core Ops, SparseCore 0:
  53.0 67.8 all-gather.2
